TPU v7x, 32 devices: a whole 2x2x4 slice. The times are simulated.
32 devices in a mesh: groups: 2 (over x), frame: 8 (over z, y), chan: 2 (over core).
Axes of the slice: x: 2, y: 2, z: 4, core: 2. Of those that a mesh axis runs over, the one named last changes fastest.
Arguments:
- frames: bfloat16 [32, 64, 128, 128], P(('groups', 'frame'), 'chan'), parts along dimension 0, may hold values from -6 to 6
- spatial_weight: bfloat16 [9, 64, 64], replicated, may hold values from -0.25 to 0.25
- spatial_bias: float32 [64], replicated, may hold values from -3 to 3
- temporal_weight: bfloat16 [3, 64, 64], replicated, may hold values from -0.4375 to 0.4375
- cotangent: bfloat16 [32, 64, 16384], P('groups', None, ('frame', 'chan')), parts along dimension 0, may hold values from -6 to 6
Outputs:
- output: bfloat16 [32, 64, 16384], P('groups', None, ('frame', 'chan')), parts along dimension 0
- grad_spatial: float32 [18, 64, 64], P('groups'), parts along dimension 0
- grad_bias: float32 [128], P('groups'), parts along dimension 0
- grad_temporal: float32 [6, 64, 64], P('groups'), parts along dimension 0
There are 2 independent parts, one for each index of `groups`. A program takes and returns all parts, laid end to end along the dimension named above; an argument that names none is the same for every part. Nothing has to cross between parts.
All inputs are finite; a program needn't handle non-finite values.
Results may differ from a plain program's by a relative error of at most 0.0055.
Values may be sent and summed in bfloat16 or wider, within the bound.
No kernel may reach another device: no remote copies, remote signals or barrier semaphores. Data moves between devices by JAX's collectives and lax.ppermute only.
A program may use at most 192 MiB of HBM per device.

v0:
```python
import math

import jax
import jax.numpy as jnp
from jax import lax
from jax.experimental import pallas as pl
from jax.experimental.pallas import tpu as pltpu
from jax.sharding import PartitionSpec as P

FRAME_DILATION = 2
BOTH = ("frame", "chan")
F32 = jnp.float32
BF16 = jnp.bfloat16
LANES_IN_LANES = (((1,), (1,)), ((), ()))


def call(
    kernel, name, out_shape, flops, scratch=(), grid=None, in_specs=None, out_specs=None, **more
):
    shapes = out_shape if isinstance(out_shape, tuple) else (out_shape,)
    nbytes = sum(2 * math.prod(s.shape) * jnp.dtype(s.dtype).itemsize for s in shapes)
    cost = pl.CostEstimate(flops=flops, transcendentals=0, bytes_accessed=nbytes)
    params = dict(out_shape=out_shape, scratch_shapes=list(scratch), name=name, **more)
    params.update(cost_estimate=cost)
    if grid is not None:
        params.update(grid=grid)
    if in_specs is not None:
        params.update(in_specs=in_specs)
    if out_specs is not None:
        params.update(out_specs=out_specs)
    return pl.pallas_call(
        kernel, compiler_params=pltpu.CompilerParams(vmem_limit_bytes=24 << 20), **params
    )


IN_HBM = pl.BlockSpec(memory_space=pltpu.HBM)
ON_CHIP = pl.BlockSpec(memory_space=pltpu.VMEM)
SCALARS = pl.BlockSpec(memory_space=pltpu.SMEM)


def pack(frames, blocks):
    local, width, height, cols = frames.shape
    rows = height // blocks
    tile = min(height, 64)
    per = tile // rows

    def kernel(images_ref, out_ref):
        for j in range(local):
            lines = jnp.swapaxes(images_ref[j], 0, 1)
            for d in range(per):
                out_ref[d, j] = lines[d * rows : (d + 1) * rows]

    return call(
        kernel,
        "pack",
        pltpu.HBM((blocks, local, rows, width, cols), frames.dtype),
        frames.size,
        grid=(height // tile,),
        in_specs=[pl.BlockSpec((local, width, tile, cols), lambda i: (0, 0, i, 0))],
        out_specs=pl.BlockSpec((per, local, rows, width, cols), lambda i: (i, 0, 0, 0, 0)),
    )(pltpu.with_memory_space_constraint(frames, pltpu.HBM))


def edge_rows(side, lines):
    owners, members, local, rows, width, cols = lines.shape
    shape = jax.ShapeDtypeStruct((owners, members, local, width, cols), lines.dtype)

    def kernel(side_ref, lines_ref, near_ref, far_ref):
        @pl.when(side_ref[0] == 0)
        def _():
            near_ref[...] = lines_ref[:, :, :, rows - 1]
            far_ref[...] = lines_ref[:, :, :, 0]

        @pl.when(side_ref[0] == 1)
        def _():
            near_ref[...] = lines_ref[:, :, :, 0]
            far_ref[...] = lines_ref[:, :, :, rows - 1]

    return call(
        kernel,
        "edge_rows",
        (shape, shape),
        lines.size,
        in_specs=[SCALARS, ON_CHIP],
        out_specs=(ON_CHIP, ON_CHIP),
    )(side, lines)


def prepare(cotangent, temporal_weight, spatial_weight, bias, cols):
    total, channels, pixels = cotangent.shape
    taps = temporal_weight.shape[0]
    lag = FRAME_DILATION
    span = min(pixels, 256)

    def kernel(cot_ref, tw_ref, sw_ref, bias_ref, out_ref, w_ref, tile_ref, ahead_s):
        for k in range(taps):
            turned = jnp.transpose(tw_ref[k].astype(F32))
            ahead_s[:, k * channels : (k + 1) * channels] = turned.astype(BF16)
        for q in range(3):
            for s in range(3):
                w_ref[s * channels : (s + 1) * channels, q * channels : (q + 1) * channels] = (
                    sw_ref[3 * q + s]
                )
        tile_ref[...] = jnp.transpose(jnp.broadcast_to(bias_ref[...], (cols, channels)))
        for t in range(total):
            here = [k for k in range(taps) if t + k * lag < total]
            weights = ahead_s[:, : len(here) * channels]
            for at in range(0, pixels, span):
                ahead = jnp.concatenate(
                    [cot_ref[t + k * lag, :, at : at + span] for k in here], axis=0
                )
                grad = jnp.dot(weights, ahead, preferred_element_type=F32)
                grad = grad + cot_ref[t, :, at : at + span].astype(F32)
                out_ref[t, :, at : at + span] = grad.astype(BF16)

    return call(
        kernel,
        "prepare",
        (
            jax.ShapeDtypeStruct(cotangent.shape, BF16),
            jax.ShapeDtypeStruct((3 * channels, 3 * channels), BF16),
            jax.ShapeDtypeStruct((channels, cols), F32),
        ),
        8 * taps * channels * cotangent.size,
        scratch=[pltpu.VMEM((channels, taps * channels), BF16)],
        in_specs=[ON_CHIP] * 4,
        out_specs=(ON_CHIP,) * 3,
    )(cotangent, temporal_weight, spatial_weight, bias)


def temporal_output(inner, outer, temporal_weight, parity, rest=None):
    total, channels, inside = inner.shape
    span = outer.shape[2]
    cols = span // 2
    count = total // 2
    pixels = inside + span
    taps = temporal_weight.shape[0]

    def kernel(*refs):
        inner_ref, outer_ref, tw_ref, out_ref, w_s = refs[0], refs[1], refs[2], refs[-2], refs[-1]
        for k in range(taps):
            w_s[:, k * channels : (k + 1) * channels] = tw_ref[k]
        for f in range(count):
            here = [k for k in range(taps) if f - k >= 0]
            weights = w_s[:, : len(here) * channels]

            def value_of(ref, at):
                delayed = jnp.concatenate(
                    [ref[f - k, 0, :, at : at + span] for k in here], axis=0
                )
                value = jnp.dot(weights, delayed, preferred_element_type=F32)
                return (value + ref[f, 0, :, at : at + span].astype(F32)).astype(BF16)

            for at in range(0, inside, span):
                out_ref[f, 0, :, cols + at : cols + at + span] = value_of(inner_ref, at)
            value = value_of(outer_ref, 0)
            out_ref[f, 0, :, :cols] = value[:, :cols]
            out_ref[f, 0, :, pixels - cols :] = value[:, cols:]

    def part(width):
        return pl.BlockSpec((count, 1, channels, width), lambda i: (0, parity, 0, 0))

    in_specs = [
        part(inside),
        part(span),
        pl.BlockSpec(temporal_weight.shape, lambda i: (0, 0, 0)),
    ]
    operands = [
        inner.reshape(count, 2, channels, inside),
        outer.reshape(count, 2, channels, span),
        temporal_weight,
    ]
    more = {}
    if rest is not None:
        in_specs.append(pl.BlockSpec(memory_space=pl.ANY))
        operands.append(rest)
        more["input_output_aliases"] = {3: 0}
    return call(
        kernel,
        "temporal_output",
        jax.ShapeDtypeStruct((count, 2, channels, pixels), BF16),
        8 * taps * channels * inner.size,
        scratch=[pltpu.VMEM((channels, taps * channels), BF16)],
        grid=(1,),
        in_specs=in_specs,
        out_specs=part(pixels),
        **more,
    )(*operands)


def gelu_and_slope(values):
    scale = 0.7978845608
    cubic = (scale * 0.044715) * (values * values)
    bent = jnp.tanh(values * (scale + cubic))
    half = 0.5 + 0.5 * bent
    active = values * half
    slope = half * (1.0 + (values - active) * (2.0 * scale + 6.0 * cubic))
    return active, slope


def layer(name, listed, lines, halo, cotangent, back_grad, weights, bias_tile, taps, sums):
    owners, members, local, rows, width, cols = lines.shape
    total = owners * local
    channels = members * width
    pixels = len(listed) * cols
    final = sums is not None
    packed = (9 + taps + 1) // 2 * channels + 16
    half = packed // 2
    trio = 3 * channels
    joined = local if pixels <= 512 else 1
    near_frames = 4
    ahead = near_frames + taps - 1
    pieces_of = []
    for at, r in enumerate(listed):
        if pieces_of and pieces_of[-1][0] + pieces_of[-1][2] == r:
            pieces_of[-1][2] += 1
        else:
            pieces_of.append([r, at, 1])

    def kernel(*refs):
        refs = list(refs)
        if halo is not None:
            side_ref, near_ref, far_ref = refs[:3]
            refs = refs[3:]
        x_ref, cot_ref, back_ref, w_ref, bias_ref = refs[:5]
        refs = refs[5:]
        if final:
            before = refs[:3]
            refs = refs[3:]
        hid_ref = refs.pop(0)
        results = refs[: 2 if final else 3]
        refs = refs[2 if final else 3 :]
        gp_s, pair_s, cot_s, back_s, cot_sems, back_sems = refs[:6]
        refs = refs[6:]

        def fetch(source, target, frames, sems):
            return [
                pltpu.make_async_copy(
                    source.at[frames, :, :, pl.ds(start * cols, count * cols)],
                    target.at[frames, :, :, pl.ds(at * cols, count * cols)],
                    sems.at[p],
                )
                for p, (start, at, count) in enumerate(pieces_of)
            ]

        back_copies = [
            fetch(back_ref, back_s, pl.ds(f, 1), back_sems.at[f]) for f in range(owners)
        ]
        cot_copies = fetch(cot_ref, cot_s, pl.ds(0, owners), cot_sems)
        for copies in back_copies + [cot_copies]:
            for copy in copies:
                copy.start()

        if halo is not None:
            top_s, bottom_s = refs[:2]
            refs = refs[2:]

            @pl.when(side_ref[0] == 0)
            def _():
                top_s[...] = far_ref[...]
                bottom_s[...] = near_ref[...]

            @pl.when(side_ref[0] == 1)
            def _():
                top_s[...] = near_ref[...]
                bottom_s[...] = far_ref[...]

        lane = lax.broadcasted_iota(jnp.int32, (channels, cols), 1)
        first = lane == 0
        last = lane == cols - 1

        def shifted(tile, by):
            if by == 1:
                return jnp.where(first, 0.0, pltpu.roll(tile, 1, 1))
            return jnp.where(last, 0.0, pltpu.roll(tile, cols - 1, 1))

        def row(f, j, r):
            if r < 0:
                return [top_s[f, c, j] for c in range(members)]
            if r == rows:
                return [bottom_s[f, c, j] for c in range(members)]
            return [x_ref[f, c, j, r] for c in range(members)]

        def three_rows(f, j, r):
            return jnp.concatenate(row(f, j, r - 1) + row(f, j, r) + row(f, j, r + 1), axis=0)

        bias_sum = None
        for f in range(owners):
            for copy in back_copies[f]:
                copy.wait()
            for j0 in range(0, local, joined):
                sources = [(j, n, r) for j in range(j0, j0 + joined) for n, r in enumerate(listed)]
                stack = jnp.concatenate([three_rows(f, j, r) for j, n, r in sources], axis=1)
                conv = jnp.dot(w_ref[...], stack, preferred_element_type=F32)
                for u, (j, n, r) in enumerate(sources):
                    lo = u * cols
                    span = slice(n * cols, n * cols + cols)
                    at = (f * local + j) * pixels + n * cols
                    place = slice(at, at + cols)
                    pre = (
                        shifted(conv[:channels, lo : lo + cols], 1)
                        + conv[channels : 2 * channels, lo : lo + cols]
                        + shifted(conv[2 * channels :, lo : lo + cols], -1)
                        + bias_ref[...]
                    )
                    active, slope = gelu_and_slope(pre)
                    hid_ref[f, j, :, span] = active.astype(BF16)
                    rounded = (back_s[f, j, :, span].astype(F32) * slope).astype(BF16)
                    grad = rounded.astype(F32)
                    bias_sum = grad if bias_sum is None else bias_sum + grad
                    gp_s[0:channels, place] = shifted(grad, -1).astype(BF16)
                    gp_s[channels : 2 * channels, place] = rounded
                    gp_s[2 * channels :, place] = shifted(grad, 1).astype(BF16)
        whole = jnp.concatenate(
            [
                three_rows(f, j, r)
                for f in range(owners)
                for j in range(local)
                for r in listed
            ],
            axis=1,
        )
        spatial = lax.dot_general(gp_s[...], whole, LANES_IN_LANES, preferred_element_type=F32)

        for copy in cot_copies:
            copy.wait()
        cot_s[pl.ds(owners, taps - 1)] = jnp.zeros((taps - 1, local, channels, pixels), BF16)
        fresh = True
        for j in range(local):
            for f in range(0, owners, near_frames):
                pairs = lax.dot_general(
                    cot_s[f : f + ahead, j].reshape(ahead * channels, pixels),
                    hid_ref[f : f + near_frames, j].reshape(near_frames * channels, pixels),
                    LANES_IN_LANES,
                    preferred_element_type=F32,
                )
                if fresh:
                    pair_s[...] = pairs
                else:
                    pair_s[...] += pairs
                fresh = False
        temporal = []
        for k in range(taps):
            block = None
            for a in range(near_frames):
                more = pair_s[
                    (a + k) * channels : (a + k + 1) * channels, a * channels : (a + 1) * channels
                ]
                block = more if block is None else block + more
            temporal.append(block)

        if final:
            gs_s, pack_s = refs
            gs_s[...] = spatial + before[0][...]
            pieces = []
            for q in range(3):
                for s in range(3):
                    pieces.append(
                        gs_s[s * channels : (s + 1) * channels, q * channels : (q + 1) * channels]
                    )
            for k in range(taps):
                pieces.append(temporal[k] + before[1][k])
            for p in range(len(pieces) // 2):
                pack_s[p * channels : (p + 1) * channels] = jnp.concatenate(
                    pieces[2 * p : 2 * p + 2], axis=1
                )
            base = len(pieces) // 2 * channels
            column = jnp.sum(jnp.transpose(bias_sum + before[2][...]), axis=0, keepdims=True)
            pack_s[base:] = jnp.zeros((packed - base, 2 * channels), F32)
            pack_s[base : base + 1, 0:channels] = column
            mine_ref, other_ref = results
            at = side_ref[0]
            mine_ref[...] = pack_s[pl.ds(pl.multiple_of(at * half, 8), half)]
            other_ref[...] = pack_s[pl.ds(pl.multiple_of((1 - at) * half, 8), half)]
        else:
            gs_ref, gt_ref, gb_ref = results
            gs_ref[...] = spatial
            for k in range(taps):
                gt_ref[k] = temporal[k]
            gb_ref[...] = bias_sum

    view = (owners, local) + cotangent.shape[1:]
    operands = [
        lines,
        pltpu.with_memory_space_constraint(cotangent.reshape(view), pltpu.HBM),
        pltpu.with_memory_space_constraint(back_grad.reshape(view), pltpu.HBM),
        weights,
        bias_tile,
    ]
    in_specs = [ON_CHIP, IN_HBM, IN_HBM, ON_CHIP, ON_CHIP]
    shapes = [jax.ShapeDtypeStruct((owners, local, channels, pixels), BF16)]
    square = (trio, trio)
    slab = (taps, channels, channels)
    tile = (channels, cols)
    scratch = [
        pltpu.VMEM((trio, total * pixels), BF16),
        pltpu.VMEM((ahead * channels, near_frames * channels), F32),
        pltpu.VMEM((owners + taps - 1, local, channels, pixels), BF16),
        pltpu.VMEM((owners, local, channels, pixels), BF16),
        pltpu.SemaphoreType.DMA((len(pieces_of),)),
        pltpu.SemaphoreType.DMA((owners, len(pieces_of))),
    ]
    if halo is not None:
        operands = list(halo) + operands
        in_specs = [SCALARS, ON_CHIP, ON_CHIP] + in_specs
        scratch += [pltpu.VMEM((owners, members, local, width, cols), BF16)] * 2
    if final:
        operands += list(sums)
        in_specs += [ON_CHIP] * 3
        shapes += [jax.ShapeDtypeStruct((half, 2 * channels), F32)] * 2
        scratch += [pltpu.VMEM(square, F32), pltpu.VMEM((packed, 2 * channels), F32)]
    else:
        shapes += [jax.ShapeDtypeStruct(s, F32) for s in (square, slab, tile)]
    hidden, *rest = call(
        kernel,
        name,
        tuple(shapes),
        8 * (2 * 9 + taps) * channels * total * channels * pixels,
        scratch=scratch,
        in_specs=in_specs,
        out_specs=tuple(ON_CHIP for _ in shapes),
    )(*operands)
    return [hidden.reshape(total, channels, pixels)] + rest


def sum_over_devices(mine, other, owners, beside, beneath):
    part = mine + lax.ppermute(other, BOTH, beside)
    bit = 1
    while bit < owners:
        part = part + lax.ppermute(part, "frame", [(i, i ^ bit) for i in range(owners)])
        if bit > 1 and beneath:
            part = beneath.pop(0)(part)
        bit *= 2
    return part


def unpack(side, mine, other, taps, channels):
    half = mine.shape[0]

    def kernel(side_ref, mine_ref, other_ref, gs_ref, gb_ref, gt_ref, pack_s):
        at = side_ref[0]
        pack_s[pl.ds(pl.multiple_of(at * half, 8), half)] = mine_ref[...]
        pack_s[pl.ds(pl.multiple_of((1 - at) * half, 8), half)] = other_ref[...]
        for n in range(9 + taps):
            p, u = n // 2, n % 2
            piece = pack_s[p * channels : (p + 1) * channels, u * channels : (u + 1) * channels]
            if n < 9:
                gs_ref[n] = piece
            else:
                gt_ref[n - 9] = piece
        base = (9 + taps) // 2 * channels
        gb_ref[...] = pack_s[base : base + 1, 0:channels]

    return call(
        kernel,
        "unpack",
        (
            jax.ShapeDtypeStruct((9, channels, channels), F32),
            jax.ShapeDtypeStruct((1, channels), F32),
            jax.ShapeDtypeStruct((taps, channels, channels), F32),
        ),
        mine.size,
        scratch=[pltpu.VMEM((2 * half, 2 * channels), F32)],
        in_specs=[SCALARS, ON_CHIP, ON_CHIP],
    )(side, mine, other)


def make_body(owners, members):
    count = owners * members
    beside = [(i, i ^ 1) for i in range(count)]
    beyond = [(i, i - 1) for i in range(2, count, 2)] + [(i, i + 1) for i in range(1, count - 1, 2)]

    def body(frames, spatial_weight, spatial_bias, temporal_weight, cotangent):
        channels = spatial_weight.shape[1]
        taps = temporal_weight.shape[0]
        cols = frames.shape[3]
        side = lax.axis_index("chan").astype(jnp.int32).reshape(1)
        lines = lax.all_to_all(pack(frames, count), BOTH, split_axis=0, concat_axis=0, tiled=True)
        lines = lines.reshape((owners, members) + lines.shape[1:])
        rows = lines.shape[3]
        back_grad, weights, bias_tile = prepare(
            cotangent, temporal_weight, spatial_weight, spatial_bias.reshape(1, channels), cols
        )
        near_row, far_row = edge_rows(side, lines)
        near = lax.ppermute(near_row, BOTH, beside)
        far = lax.ppermute(far_row, BOTH, beyond)
        shared = (cotangent, back_grad, weights, bias_tile, taps)
        inside = list(range(1, rows - 1))
        inner, *sums = layer("layer_inside", inside, lines, None, *shared, None)
        halo = (side, near, far)
        outer, mine, other = layer("layer_edges", [0, rows - 1], lines, halo, *shared, sums)
        made = []

        def output_of(parity):
            def step(part):
                value = temporal_output(inner, outer, temporal_weight, parity, *made)
                part, value = lax.optimization_barrier((part, value))
                made[:] = [value]
                return part

            return step

        part = sum_over_devices(mine, other, owners, beside, [output_of(0), output_of(1)])
        rest = lax.ppermute(part, BOTH, beside)
        grad_spatial, grad_bias, grad_temporal = unpack(side, part, rest, taps, channels)
        return (
            made[0].reshape(cotangent.shape),
            grad_spatial,
            grad_bias.reshape(channels),
            grad_temporal,
        )

    return body


def solution(mesh):
    return jax.shard_map(
        make_body(mesh.shape["frame"], mesh.shape["chan"]),
        mesh=mesh,
        in_specs=(
            P(("groups", "frame"), "chan", None, None),
            P(),
            P(),
            P(),
            P("groups", None, ("frame", "chan")),
        ),
        out_specs=(
            P("groups", None, ("frame", "chan")),
            P("groups", None, None),
            P("groups"),
            P("groups", None, None),
        ),
        check_vma=False,
    )
```

profile of v0, /device:TPU:0, one launch (start us, length us, event | category | flops | bytes accessed | tf_op | source)
XLA Modules:
  0.0 97.1 jit_solution(12457120896930157441)
XLA Ops:
  0.6 2.9 %pack.1 = bf16[16,2,8,32,128]{4,3,2,1,0:T(8,128)(2,1)} custom-call(bf16[2,32,128,128]{3,2,1,0:T(8,128)(2,1)} %images_ref.1), custom_call_target="tpu_custom_call" | custom-call | flops 1048576 | bytes 4194304 | tf_op jit(solution)/shard_map/pack/pallas_call | solution.py:53
  3.5 0.0 copy-start
  3.5 0.0 copy-start.2
  3.5 0.0 copy-start.3
  3.5 7.5 %all-to-all-start = ((bf16[16,2,8,32,128]{4,3,2,1,0:T(8,128)(2,1)}), bf16[16,2,8,32,128]{4,3,2,1,0:T(8,128)(2,1)S(1)}, u32[]{:S(2)}, u32[]{:S(2)}) async-start(bf16[16,2,8,32,128]{4,3,2,1,0:T(8,128)(2,1)} %pack.1), calls=%async_computation | async-start | bytes 4194304 | tf_op jit(solution)/shard_map/all_to_all | solution.py:478
  11.1 0.0 copy-done
  11.1 0.0 copy-done.2
  11.1 0.0 copy-done.3
  11.1 0.0 copy-start.1
  11.1 1.6 %copy-done.1 = bf16[16,64,1024]{2,1,0:T(8,128)(2,1)S(1)} copy-done((bf16[16,64,1024]{2,1,0:T(8,128)(2,1)S(1)}, bf16[16,64,1024]{2,1,0:T(8,128)(2,1)}, u32[]{:S(2)}) %copy-start.1) | copy-done | bytes 2097176
  12.7 1.3 %prepare.1 = (bf16[16,64,1024]{2,1,0:T(8,128)(2,1)S(1)}, bf16[192,192]{1,0:T(8,128)(2,1)S(1)}, f32[64,128]{1,0:T(8,128)S(1)}) custom-call(bf16[16,64,1024]{2,1,0:T(8,128)(2,1)S(1)} %copy-done.1, bf16[3,64,64]{2,1,0:T(8,128)(2,1)S(1)} %copy-done, bf16[9,64,64]{2,1,0:T(8,128)(2,1)S(1)} %copy-done.2, f32[1,64]{1,0:T(1,128)S(1)} %bitcast.12), custom_call_target="tpu_custom_call" | custom-call | flops 1610612736 | bytes 4407296 | tf_op jit(solution)/shard_map/prepare/pallas_call | solution.py:116
  14.0 0.0 copy-start.4
  14.0 1.3 %copy-done.4 = bf16[16,64,1024]{2,1,0:T(8,128)(2,1)} copy-done((bf16[16,64,1024]{2,1,0:T(8,128)(2,1)}, bf16[16,64,1024]{2,1,0:T(8,128)(2,1)S(1)}, u32[]{:S(2)}) %copy-start.4) | copy-done | bytes 2097176
  15.4 36.8 %all-to-all-done = bf16[16,2,8,32,128]{4,3,2,1,0:T(8,128)(2,1)S(1)} async-done(((bf16[16,2,8,32,128]{4,3,2,1,0:T(8,128)(2,1)}), bf16[16,2,8,32,128]{4,3,2,1,0:T(8,128)(2,1)S(1)}, u32[]{:S(2)}, u32[]{:S(2)}) %all-to-all-start) | async-done | bytes 2097184 | tf_op jit(solution)/shard_map/all_to_all | solution.py:478
  52.2 0.8 collective-permute-start
  53.0 0.7 collective-permute-start.1
  53.7 10.3 %layer_inside.1 = (bf16[8,2,64,768]{3,2,1,0:T(8,128)(2,1)S(1)}, f32[192,192]{1,0:T(8,128)S(1)}, f32[3,64,64]{2,1,0:T(8,128)S(1)}, f32[64,128]{1,0:T(8,128)S(1)}) custom-call(bf16[8,2,2,8,32,128]{5,4,3,2,1,0:T(8,128)(2,1)S(1)} %bitcast.8, bf16[8,2,64,1024]{3,2,1,0:T(8,128)(2,1)} %bitcast.10, bf16[8,2,64,1024]{3,2,1,0:T(8,128)(2,1)} %bitcast.13, ...), custom_call_target="tpu_custom_call" | custom-call | flops 8455716864 | bytes 3604480 | tf_op jit(solution)/shard_map/layer_inside/pallas_call | solution.py:414
  64.1 0.0 collective-permute-done.refs_1_
  64.1 0.0 collective-permute-done.1.refs_2_
  64.1 5.7 %layer_edges.1 = (bf16[8,2,64,256]{3,2,1,0:T(8,128)(2,1)S(1)}, f32[200,128]{1,0:T(8,128)S(1)}, f32[200,128]{1,0:T(8,128)S(1)}) custom-call(s32[1]{0:T(128)} %bitcast.side_ref.refs_0_, bf16[8,2,2,32,128]{4,3,2,1,0:T(8,128)(2,1)S(1)} %collective-permute-done.refs_1_, bf16[8,2,2,32,128]{4,3,2,1,0:T(8,128)(2,1)S(1)} %collective-permute-done.1.refs_2_, ...), custom_call_target="tpu_custom_call" | custom-call | flops 2818572288 | bytes 1458176 | tf_op jit(solution)/shard_map/layer_edges/pallas_call | solution.py:414
  69.8 4.8 %collective-permute-start.2 = (f32[200,128]{1,0:T(8,128)S(1)}, f32[200,128]{1,0:T(8,128)S(1)}, u32[]{:S(2)}, u32[]{:S(2)}) collective-permute-start(f32[200,128]{1,0:T(8,128)S(1)} %get-tuple-element.32), channel_id=1, source_target_pairs={{0,1},{1,0},{2,3},{3,2},{4,5},{5,4},{6,7},{7,6},{8,9},{9,8},{10,11... | collective-permute-start | bytes 307208 | tf_op jit(solution)/shard_map/ppermute | solution.py:427
  74.6 0.9 collective-permute-done.2
  75.5 4.4 %collective-permute-start.3 = (f32[200,128]{1,0:T(8,128)S(1)}, f32[200,128]{1,0:T(8,128)S(1)}, u32[]{:S(2)}, u32[]{:S(2)}) collective-permute-start(f32[200,128]{1,0:T(8,128)S(1)} %add.12), channel_id=1, source_target_pairs={{0,2},{2,0},{4,6},{6,4},{8,10},{10,8},{12,14},{14,12},{1,3},{3,1},... | collective-permute-start | bytes 307208 | tf_op jit(solution)/shard_map/ppermute | solution.py:430
  79.9 3.4 %collective-permute-done.3 = f32[200,128]{1,0:T(8,128)S(1)} collective-permute-done((f32[200,128]{1,0:T(8,128)S(1)}, f32[200,128]{1,0:T(8,128)S(1)}, u32[]{:S(2)}, u32[]{:S(2)}) %collective-permute-start.3) | collective-permute-done | bytes 102432 | tf_op jit(solution)/shard_map/ppermute | solution.py:430
  83.3 3.2 %collective-permute-start.4 = (f32[200,128]{1,0:T(8,128)S(1)}, f32[200,128]{1,0:T(8,128)S(1)}, u32[]{:S(2)}, u32[]{:S(2)}) collective-permute-start(f32[200,128]{1,0:T(8,128)S(1)} %add.13), channel_id=1, source_target_pairs={{0,4},{2,6},{4,0},{6,2},{8,12},{10,14},{12,8},{14,10},{1,5},{3,7},... | collective-permute-start | bytes 307208 | tf_op jit(solution)/shard_map/ppermute | solution.py:430
  86.5 1.7 %temporal_output.2.refs_3_ = bf16[8,2,64,1024]{3,2,1,0:T(8,128)(2,1)} custom-call(bf16[8,2,64,768]{3,2,1,0:T(8,128)(2,1)S(1)} %get-tuple-element.33.refs_0_, bf16[8,2,64,256]{3,2,1,0:T(8,128)(2,1)S(1)} %get-tuple-element.34.refs_1_, bf16[3,64,64]{2,1,0:T(8,128)(2,1)S(1)} %copy-done), custom_call_target="tpu_custom_call" | custom-call | flops 1207959552 | bytes 4194304 | tf_op jit(solution)/shard_map/temporal_output/pallas_call | solution.py:178
  88.2 1.0 collective-permute-done.4
  89.2 2.8 %collective-permute-start.5 = (f32[200,128]{1,0:T(8,128)S(1)}, f32[200,128]{1,0:T(8,128)S(1)}, u32[]{:S(2)}, u32[]{:S(2)}) collective-permute-start(f32[200,128]{1,0:T(8,128)S(1)} %add.14), channel_id=1, source_target_pairs={{0,8},{2,10},{4,12},{6,14},{8,0},{10,2},{12,4},{14,6},{1,9},{3,11}... | collective-permute-start | bytes 307208 | tf_op jit(solution)/shard_map/ppermute | solution.py:430
  92.0 1.7 %temporal_output.3 = bf16[8,2,64,1024]{3,2,1,0:T(8,128)(2,1)} custom-call(bf16[8,2,64,768]{3,2,1,0:T(8,128)(2,1)S(1)} %get-tuple-element.33.refs_0_, bf16[8,2,64,256]{3,2,1,0:T(8,128)(2,1)S(1)} %get-tuple-element.34.refs_1_, bf16[3,64,64]{2,1,0:T(8,128)(2,1)S(1)} %copy-done, ...), custom_call_target="tpu_custom_call", output_to_operand_aliasing={{}: (3, {})} | custom-call | flops 1207959552 | bytes 4194304 | tf_op jit(solution)/shard_map/temporal_output/pallas_call | solution.py:178
  93.7 1.1 %collective-permute-done.5 = f32[200,128]{1,0:T(8,128)S(1)} collective-permute-done((f32[200,128]{1,0:T(8,128)S(1)}, f32[200,128]{1,0:T(8,128)S(1)}, u32[]{:S(2)}, u32[]{:S(2)}) %collective-permute-start.5) | collective-permute-done | bytes 102432 | tf_op jit(solution)/shard_map/ppermute | solution.py:430
  94.8 0.1 collective-permute-start.6
  94.9 1.3 %collective-permute-done.6.other_ref = f32[200,128]{1,0:T(8,128)S(1)} collective-permute-done((f32[200,128]{1,0:T(8,128)S(1)}, f32[200,128]{1,0:T(8,128)S(1)}, u32[]{:S(2)}, u32[]{:S(2)}) %collective-permute-start.6) | collective-permute-done | bytes 102432 | tf_op jit(solution)/shard_map/ppermute | solution.py:504
  96.2 0.9 unpack.1
  (5 shorter events, 0.1 us)
Async XLA Ops:
  3.5 7.5 %copy-start = (bf16[3,64,64]{2,1,0:T(8,128)(2,1)S(1)}, bf16[3,64,64]{2,1,0:T(8,128)(2,1)}, u32[]{:S(2)}) copy-start(bf16[3,64,64]{2,1,0:T(8,128)(2,1)} %refs_2_.3) | copy-start | bytes 73732
  3.5 7.6 %copy-start.2 = (bf16[9,64,64]{2,1,0:T(8,128)(2,1)S(1)}, bf16[9,64,64]{2,1,0:T(8,128)(2,1)}, u32[]{:S(2)}) copy-start(bf16[9,64,64]{2,1,0:T(8,128)(2,1)} %sw_ref.1) | copy-start | bytes 221188
  3.5 7.6 %copy-start.3 = (f32[64]{0:T(128)S(1)}, f32[64]{0:T(128)}, u32[]{:S(2)}) copy-start(f32[64]{0:T(128)} %param.7) | copy-start | bytes 772
  3.5 48.6 %all-to-all-start = ((bf16[16,2,8,32,128]{4,3,2,1,0:T(8,128)(2,1)}), bf16[16,2,8,32,128]{4,3,2,1,0:T(8,128)(2,1)S(1)}, u32[]{:S(2)}, u32[]{:S(2)}) async-start(bf16[16,2,8,32,128]{4,3,2,1,0:T(8,128)(2,1)} %pack.1), calls=%async_computation | async-start | bytes 4194304 | tf_op jit(solution)/shard_map/all_to_all | solution.py:478
  11.1 1.6 %copy-start.1 = (bf16[16,64,1024]{2,1,0:T(8,128)(2,1)S(1)}, bf16[16,64,1024]{2,1,0:T(8,128)(2,1)}, u32[]{:S(2)}) copy-start(bf16[16,64,1024]{2,1,0:T(8,128)(2,1)} %cot_ref.1) | copy-start | bytes 6291460
  14.0 1.3 %copy-start.4 = (bf16[16,64,1024]{2,1,0:T(8,128)(2,1)}, bf16[16,64,1024]{2,1,0:T(8,128)(2,1)S(1)}, u32[]{:S(2)}) copy-start(bf16[16,64,1024]{2,1,0:T(8,128)(2,1)S(1)} %get-tuple-element.25) | copy-start | bytes 6291460
  52.2 11.9 %collective-permute-start = (bf16[8,2,2,32,128]{4,3,2,1,0:T(8,128)(2,1)S(1)}, bf16[8,2,2,32,128]{4,3,2,1,0:T(8,128)(2,1)S(1)}, u32[]{:S(2)}, u32[]{:S(2)}) collective-permute-start(bf16[8,2,2,32,128]{4,3,2,1,0:T(8,128)(2,1)S(1)} %get-tuple-element.23), channel_id=1, source_target_pairs={{0,1},{1,0},{2,3},{3,2},{4,5},{5,4},{6,7},{7,6},{8,9},{9,8},{10,11... | collective-permute-start | bytes 786440 | tf_op jit(solution)/shard_map/ppermute | solution.py:485
  53.0 11.0 %collective-permute-start.1 = (bf16[8,2,2,32,128]{4,3,2,1,0:T(8,128)(2,1)S(1)}, bf16[8,2,2,32,128]{4,3,2,1,0:T(8,128)(2,1)S(1)}, u32[]{:S(2)}, u32[]{:S(2)}) collective-permute-start(bf16[8,2,2,32,128]{4,3,2,1,0:T(8,128)(2,1)S(1)} %get-tuple-element.24), channel_id=1, source_target_pairs={{2,1},{4,3},{6,5},{8,7},{10,9},{12,11},{14,13},{1,2},{3,4},{5,6},{... | collective-permute-start | bytes 786440 | tf_op jit(solution)/shard_map/ppermute | solution.py:486
  69.8 5.7 %collective-permute-start.2 = (f32[200,128]{1,0:T(8,128)S(1)}, f32[200,128]{1,0:T(8,128)S(1)}, u32[]{:S(2)}, u32[]{:S(2)}) collective-permute-start(f32[200,128]{1,0:T(8,128)S(1)} %get-tuple-element.32), channel_id=1, source_target_pairs={{0,1},{1,0},{2,3},{3,2},{4,5},{5,4},{6,7},{7,6},{8,9},{9,8},{10,11... | collective-permute-start | bytes 307208 | tf_op jit(solution)/shard_map/ppermute | solution.py:427
  75.5 7.7 %collective-permute-start.3 = (f32[200,128]{1,0:T(8,128)S(1)}, f32[200,128]{1,0:T(8,128)S(1)}, u32[]{:S(2)}, u32[]{:S(2)}) collective-permute-start(f32[200,128]{1,0:T(8,128)S(1)} %add.12), channel_id=1, source_target_pairs={{0,2},{2,0},{4,6},{6,4},{8,10},{10,8},{12,14},{14,12},{1,3},{3,1},... | collective-permute-start | bytes 307208 | tf_op jit(solution)/shard_map/ppermute | solution.py:430
  83.3 5.9 %collective-permute-start.4 = (f32[200,128]{1,0:T(8,128)S(1)}, f32[200,128]{1,0:T(8,128)S(1)}, u32[]{:S(2)}, u32[]{:S(2)}) collective-permute-start(f32[200,128]{1,0:T(8,128)S(1)} %add.13), channel_id=1, source_target_pairs={{0,4},{2,6},{4,0},{6,2},{8,12},{10,14},{12,8},{14,10},{1,5},{3,7},... | collective-permute-start | bytes 307208 | tf_op jit(solution)/shard_map/ppermute | solution.py:430
  89.2 5.6 %collective-permute-start.5 = (f32[200,128]{1,0:T(8,128)S(1)}, f32[200,128]{1,0:T(8,128)S(1)}, u32[]{:S(2)}, u32[]{:S(2)}) collective-permute-start(f32[200,128]{1,0:T(8,128)S(1)} %add.14), channel_id=1, source_target_pairs={{0,8},{2,10},{4,12},{6,14},{8,0},{10,2},{12,4},{14,6},{1,9},{3,11}... | collective-permute-start | bytes 307208 | tf_op jit(solution)/shard_map/ppermute | solution.py:430
  94.8 1.4 %collective-permute-start.6 = (f32[200,128]{1,0:T(8,128)S(1)}, f32[200,128]{1,0:T(8,128)S(1)}, u32[]{:S(2)}, u32[]{:S(2)}) collective-permute-start(f32[200,128]{1,0:T(8,128)S(1)} %add.15.mine_ref), channel_id=1, source_target_pairs={{0,1},{1,0},{2,3},{3,2},{4,5},{5,4},{6,7},{7,6},{8,9},{9,8},{10,11... | collective-permute-start | bytes 307208 | tf_op jit(solution)/shard_map/ppermute | solution.py:504
where the time goes:
time: 97.3 us; the launch traced here: 97.1 us
  waiting for transfers between devices  44.5 us (46%)
  Pallas kernels  24.5 us (25%)
  starting transfers between devices  24.3 us (25%)
  local copies, waits for them, and re-layouts  2.93 us (3%)
    all_to_all x1, waiting for transfers between devices, body(): lax.all_to_all(pack(frames, count), BOTH, split_axis=0, concat_axis=0, ti...  36.8 us
    pallas_call x2, Pallas kernels, layer(): call(kernel, name, tuple(shapes), 8 * (2 * 9 + taps) * channels * total *...  16 us
    ppermute x3, starting transfers between devices, sum_over_devices(): lax.ppermute(part, 'frame', [(i, i ^ bit) for i in range(owners)])  10.4 us
    all_to_all x1, starting transfers between devices, body(): lax.all_to_all(pack(frames, count), BOTH, split_axis=0, concat_axis=0, ti...  7.52 us
    ppermute x3, waiting for transfers between devices, sum_over_devices(): lax.ppermute(part, 'frame', [(i, i ^ bit) for i in range(owners)])  5.46 us
    ppermute x1, starting transfers between devices, sum_over_devices(): part = mine + lax.ppermute(other, BOTH, beside)  4.79 us
    pallas_call x2, Pallas kernels, temporal_output(): call(kernel, 'temporal_output', jax.ShapeDtypeStruct((count, 2, channels,...  3.35 us
    unnamed x10, local copies, waits for them, and re-layouts  2.93 us
  transfers between devices with their start and end apart: 8, of which 6 were waited for; matrix products, arithmetic and copies ran while one was open for 0% of the time, Pallas kernels for 15%

commit v1 on v0

--- a/solution.py
+++ b/solution.py
@@ -8,6 +8,9 @@
 from jax.sharding import PartitionSpec as P
 
 FRAME_DILATION = 2
+INSIDE_FRAMES = 8
+EDGE_FRAMES = 8
+PACK_ROWS = 16
 BOTH = ("frame", "chan")
 F32 = jnp.float32
 BF16 = jnp.bfloat16
@@ -41,23 +44,47 @@
 def pack(frames, blocks):
     local, width, height, cols = frames.shape
     rows = height // blocks
-    tile = min(height, 64)
+    tile = PACK_ROWS
     per = tile // rows
-
-    def kernel(images_ref, out_ref):
-        for j in range(local):
-            lines = jnp.swapaxes(images_ref[j], 0, 1)
-            for d in range(per):
-                out_ref[d, j] = lines[d * rows : (d + 1) * rows]
+    shape = (blocks, local, rows, width, cols)
+
+    def kernel(images_ref, out_ref, images_s, lines_s, in_sems, out_sems):
+        def fetch(i):
+            part = pl.ds(i * tile, tile)
+            return pltpu.make_async_copy(
+                images_ref.at[:, :, part], images_s.at[:, :, part], in_sems.at[i]
+            )
+
+        def ship(i):
+            part = pl.ds(i * per, per)
+            return pltpu.make_async_copy(lines_s.at[part], out_ref.at[part], out_sems.at[i])
+
+        steps = range(height // tile)
+        for i in steps:
+            fetch(i).start()
+        for i in steps:
+            fetch(i).wait()
+            for j in range(local):
+                lines = jnp.swapaxes(images_s[j, :, i * tile : (i + 1) * tile], 0, 1)
+                for d in range(per):
+                    lines_s[i * per + d, j] = lines[d * rows : (d + 1) * rows]
+            ship(i).start()
+        for i in steps:
+            ship(i).wait()
 
     return call(
         kernel,
         "pack",
-        pltpu.HBM((blocks, local, rows, width, cols), frames.dtype),
+        pltpu.HBM(shape, frames.dtype),
         frames.size,
-        grid=(height // tile,),
-        in_specs=[pl.BlockSpec((local, width, tile, cols), lambda i: (0, 0, i, 0))],
-        out_specs=pl.BlockSpec((per, local, rows, width, cols), lambda i: (i, 0, 0, 0, 0)),
+        scratch=[
+            pltpu.VMEM(frames.shape, frames.dtype),
+            pltpu.VMEM(shape, frames.dtype),
+            pltpu.SemaphoreType.DMA((height // tile,)),
+            pltpu.SemaphoreType.DMA((height // tile,)),
+        ],
+        in_specs=[IN_HBM],
+        out_specs=IN_HBM,
     )(pltpu.with_memory_space_constraint(frames, pltpu.HBM))
 
 
@@ -93,39 +120,58 @@
     span = min(pixels, 256)
 
     def kernel(cot_ref, tw_ref, sw_ref, bias_ref, out_ref, w_ref, tile_ref, ahead_s):
-        for k in range(taps):
-            turned = jnp.transpose(tw_ref[k].astype(F32))
-            ahead_s[:, k * channels : (k + 1) * channels] = turned.astype(BF16)
-        for q in range(3):
-            for s in range(3):
-                w_ref[s * channels : (s + 1) * channels, q * channels : (q + 1) * channels] = (
-                    sw_ref[3 * q + s]
-                )
-        tile_ref[...] = jnp.transpose(jnp.broadcast_to(bias_ref[...], (cols, channels)))
+        @pl.when(pl.program_id(0) == 0)
+        def _():
+            for k in range(taps):
+                turned = jnp.transpose(tw_ref[k].astype(F32))
+                ahead_s[:, k * channels : (k + 1) * channels] = turned.astype(BF16)
+            for q in range(3):
+                for s in range(3):
+                    w_ref[s * channels : (s + 1) * channels, q * channels : (q + 1) * channels] = (
+                        sw_ref[3 * q + s]
+                    )
+            tile_ref[...] = jnp.transpose(jnp.broadcast_to(bias_ref[...], (cols, channels)))
+
         for t in range(total):
             here = [k for k in range(taps) if t + k * lag < total]
             weights = ahead_s[:, : len(here) * channels]
-            for at in range(0, pixels, span):
-                ahead = jnp.concatenate(
-                    [cot_ref[t + k * lag, :, at : at + span] for k in here], axis=0
-                )
-                grad = jnp.dot(weights, ahead, preferred_element_type=F32)
-                grad = grad + cot_ref[t, :, at : at + span].astype(F32)
-                out_ref[t, :, at : at + span] = grad.astype(BF16)
-
+            ahead = jnp.concatenate([cot_ref[t + k * lag] for k in here], axis=0)
+            grad = jnp.dot(weights, ahead, preferred_element_type=F32)
+            out_ref[t] = (grad + cot_ref[t].astype(F32)).astype(BF16)
+
+    def fixed(shape):
+        return pl.BlockSpec(shape, lambda n: (0,) * len(shape))
+
+    trio = (3 * channels, 3 * channels)
+    part = pl.BlockSpec((total, channels, span), lambda n: (0, 0, n))
     return call(
         kernel,
         "prepare",
         (
-            jax.ShapeDtypeStruct(cotangent.shape, BF16),
-            jax.ShapeDtypeStruct((3 * channels, 3 * channels), BF16),
+            pltpu.HBM(cotangent.shape, BF16),
+            jax.ShapeDtypeStruct(trio, BF16),
             jax.ShapeDtypeStruct((channels, cols), F32),
         ),
         8 * taps * channels * cotangent.size,
         scratch=[pltpu.VMEM((channels, taps * channels), BF16)],
-        in_specs=[ON_CHIP] * 4,
-        out_specs=(ON_CHIP,) * 3,
-    )(cotangent, temporal_weight, spatial_weight, bias)
+        grid=(pixels // span,),
+        in_specs=[
+            part,
+            fixed(temporal_weight.shape),
+            fixed(spatial_weight.shape),
+            fixed(bias.shape),
+        ],
+        out_specs=(
+            part,
+            fixed(trio),
+            fixed((channels, cols)),
+        ),
+    )(
+        pltpu.with_memory_space_constraint(cotangent, pltpu.HBM),
+        temporal_weight,
+        spatial_weight,
+        bias,
+    )
 
 
 def temporal_output(inner, outer, temporal_weight, parity, rest=None):
@@ -198,7 +244,7 @@
     return active, slope
 
 
-def layer(name, listed, lines, halo, cotangent, back_grad, weights, bias_tile, taps, sums):
+def layer(name, listed, lines, halo, cotangent, back_grad, weights, bias_tile, taps, sums, per):
     owners, members, local, rows, width, cols = lines.shape
     total = owners * local
     channels = members * width
@@ -216,7 +262,6 @@
             pieces_of[-1][2] += 1
         else:
             pieces_of.append([r, at, 1])
-
     def kernel(*refs):
         refs = list(refs)
         if halo is not None:
@@ -230,26 +275,18 @@
         hid_ref = refs.pop(0)
         results = refs[: 2 if final else 3]
         refs = refs[2 if final else 3 :]
-        gp_s, pair_s, cot_s, back_s, cot_sems, back_sems = refs[:6]
+        gp_s, pair_s, gs_s, gb_s, cot_s, cot_sems = refs[:6]
         refs = refs[6:]
-
-        def fetch(source, target, frames, sems):
-            return [
-                pltpu.make_async_copy(
-                    source.at[frames, :, :, pl.ds(start * cols, count * cols)],
-                    target.at[frames, :, :, pl.ds(at * cols, count * cols)],
-                    sems.at[p],
-                )
-                for p, (start, at, count) in enumerate(pieces_of)
-            ]
-
-        back_copies = [
-            fetch(back_ref, back_s, pl.ds(f, 1), back_sems.at[f]) for f in range(owners)
+        cot_copies = [
+            pltpu.make_async_copy(
+                cot_ref.at[:, :, :, pl.ds(start * cols, count * cols)],
+                cot_s.at[:, :, :, pl.ds(at * cols, count * cols)],
+                cot_sems.at[p],
+            )
+            for p, (start, at, count) in enumerate(pieces_of)
         ]
-        cot_copies = fetch(cot_ref, cot_s, pl.ds(0, owners), cot_sems)
-        for copies in back_copies + [cot_copies]:
-            for copy in copies:
-                copy.start()
+        for copy in cot_copies:
+            copy.start()
 
         if halo is not None:
             top_s, bottom_s = refs[:2]
@@ -284,61 +321,73 @@
         def three_rows(f, j, r):
             return jnp.concatenate(row(f, j, r - 1) + row(f, j, r) + row(f, j, r + 1), axis=0)
 
-        bias_sum = None
-        for f in range(owners):
-            for copy in back_copies[f]:
-                copy.wait()
-            for j0 in range(0, local, joined):
-                sources = [(j, n, r) for j in range(j0, j0 + joined) for n, r in enumerate(listed)]
-                stack = jnp.concatenate([three_rows(f, j, r) for j, n, r in sources], axis=1)
-                conv = jnp.dot(w_ref[...], stack, preferred_element_type=F32)
-                for u, (j, n, r) in enumerate(sources):
-                    lo = u * cols
-                    span = slice(n * cols, n * cols + cols)
-                    at = (f * local + j) * pixels + n * cols
-                    place = slice(at, at + cols)
-                    pre = (
-                        shifted(conv[:channels, lo : lo + cols], 1)
-                        + conv[channels : 2 * channels, lo : lo + cols]
-                        + shifted(conv[2 * channels :, lo : lo + cols], -1)
-                        + bias_ref[...]
-                    )
-                    active, slope = gelu_and_slope(pre)
-                    hid_ref[f, j, :, span] = active.astype(BF16)
-                    rounded = (back_s[f, j, :, span].astype(F32) * slope).astype(BF16)
-                    grad = rounded.astype(F32)
-                    bias_sum = grad if bias_sum is None else bias_sum + grad
-                    gp_s[0:channels, place] = shifted(grad, -1).astype(BF16)
-                    gp_s[channels : 2 * channels, place] = rounded
-                    gp_s[2 * channels :, place] = shifted(grad, 1).astype(BF16)
-        whole = jnp.concatenate(
-            [
-                three_rows(f, j, r)
-                for f in range(owners)
-                for j in range(local)
-                for r in listed
-            ],
-            axis=1,
-        )
-        spatial = lax.dot_general(gp_s[...], whole, LANES_IN_LANES, preferred_element_type=F32)
+        if final:
+            gs_s[...] = before[0][...]
+            gb_s[...] = before[2][...]
+        else:
+            gs_s[...] = jnp.zeros_like(gs_s)
+            gb_s[...] = jnp.zeros_like(gb_s)
+
+        def some_frames(i, carry):
+            bias_sum = None
+            for p in range(per):
+                f = i * per + p
+                for j0 in range(0, local, joined):
+                    sources = [
+                        (j, n, r) for j in range(j0, j0 + joined) for n, r in enumerate(listed)
+                    ]
+                    stack = jnp.concatenate([three_rows(f, j, r) for j, n, r in sources], axis=1)
+                    conv = jnp.dot(w_ref[...], stack, preferred_element_type=F32)
+                    for u, (j, n, r) in enumerate(sources):
+                        lo = u * cols
+                        span = slice(n * cols, n * cols + cols)
+                        at = (p * local + j) * pixels + n * cols
+                        place = slice(at, at + cols)
+                        pre = (
+                            shifted(conv[:channels, lo : lo + cols], 1)
+                            + conv[channels : 2 * channels, lo : lo + cols]
+                            + shifted(conv[2 * channels :, lo : lo + cols], -1)
+                            + bias_ref[...]
+                        )
+                        active, slope = gelu_and_slope(pre)
+                        hid_ref[f, j, :, span] = active.astype(BF16)
+                        back = back_ref[f, j, :, r * cols : (r + 1) * cols].astype(F32)
+                        rounded = (back * slope).astype(BF16)
+                        grad = rounded.astype(F32)
+                        bias_sum = grad if bias_sum is None else bias_sum + grad
+                        gp_s[0:channels, place] = shifted(grad, -1).astype(BF16)
+                        gp_s[channels : 2 * channels, place] = rounded
+                        gp_s[2 * channels :, place] = shifted(grad, 1).astype(BF16)
+            gb_s[...] += bias_sum
+            whole = jnp.concatenate(
+                [
+                    three_rows(i * per + p, j, r)
+                    for p in range(per)
+                    for j in range(local)
+                    for r in listed
+                ],
+                axis=1,
+            )
+            gs_s[...] += lax.dot_general(
+                gp_s[...], whole, LANES_IN_LANES, preferred_element_type=F32
+            )
+            return carry
+
+        lax.fori_loop(0, owners // per, some_frames, 0)
 
         for copy in cot_copies:
             copy.wait()
-        cot_s[pl.ds(owners, taps - 1)] = jnp.zeros((taps - 1, local, channels, pixels), BF16)
-        fresh = True
+        pair_s[...] = jnp.zeros_like(pair_s)
         for j in range(local):
             for f in range(0, owners, near_frames):
+                count = min(ahead, owners - f)
                 pairs = lax.dot_general(
-                    cot_s[f : f + ahead, j].reshape(ahead * channels, pixels),
+                    cot_s[f : f + count, j].reshape(count * channels, pixels),
                     hid_ref[f : f + near_frames, j].reshape(near_frames * channels, pixels),
                     LANES_IN_LANES,
                     preferred_element_type=F32,
                 )
-                if fresh:
-                    pair_s[...] = pairs
-                else:
-                    pair_s[...] += pairs
-                fresh = False
+                pair_s[0 : count * channels] += pairs
         temporal = []
         for k in range(taps):
             block = None
@@ -350,8 +399,7 @@
             temporal.append(block)
 
         if final:
-            gs_s, pack_s = refs
-            gs_s[...] = spatial + before[0][...]
+            (pack_s,) = refs
             pieces = []
             for q in range(3):
                 for s in range(3):
@@ -365,7 +413,7 @@
                     pieces[2 * p : 2 * p + 2], axis=1
                 )
             base = len(pieces) // 2 * channels
-            column = jnp.sum(jnp.transpose(bias_sum + before[2][...]), axis=0, keepdims=True)
+            column = jnp.sum(jnp.transpose(gb_s[...]), axis=0, keepdims=True)
             pack_s[base:] = jnp.zeros((packed - base, 2 * channels), F32)
             pack_s[base : base + 1, 0:channels] = column
             mine_ref, other_ref = results
@@ -374,31 +422,31 @@
             other_ref[...] = pack_s[pl.ds(pl.multiple_of((1 - at) * half, 8), half)]
         else:
             gs_ref, gt_ref, gb_ref = results
-            gs_ref[...] = spatial
+            gs_ref[...] = gs_s[...]
             for k in range(taps):
                 gt_ref[k] = temporal[k]
-            gb_ref[...] = bias_sum
+            gb_ref[...] = gb_s[...]
 
     view = (owners, local) + cotangent.shape[1:]
     operands = [
         lines,
         pltpu.with_memory_space_constraint(cotangent.reshape(view), pltpu.HBM),
-        pltpu.with_memory_space_constraint(back_grad.reshape(view), pltpu.HBM),
+        back_grad.reshape(view),
         weights,
         bias_tile,
     ]
-    in_specs = [ON_CHIP, IN_HBM, IN_HBM, ON_CHIP, ON_CHIP]
+    in_specs = [ON_CHIP, IN_HBM, ON_CHIP, ON_CHIP, ON_CHIP]
     shapes = [jax.ShapeDtypeStruct((owners, local, channels, pixels), BF16)]
     square = (trio, trio)
     slab = (taps, channels, channels)
     tile = (channels, cols)
     scratch = [
-        pltpu.VMEM((trio, total * pixels), BF16),
+        pltpu.VMEM((trio, per * local * pixels), BF16),
         pltpu.VMEM((ahead * channels, near_frames * channels), F32),
-        pltpu.VMEM((owners + taps - 1, local, channels, pixels), BF16),
+        pltpu.VMEM(square, F32),
+        pltpu.VMEM(tile, F32),
         pltpu.VMEM((owners, local, channels, pixels), BF16),
         pltpu.SemaphoreType.DMA((len(pieces_of),)),
-        pltpu.SemaphoreType.DMA((owners, len(pieces_of))),
     ]
     if halo is not None:
         operands = list(halo) + operands
@@ -408,7 +456,7 @@
         operands += list(sums)
         in_specs += [ON_CHIP] * 3
         shapes += [jax.ShapeDtypeStruct((half, 2 * channels), F32)] * 2
-        scratch += [pltpu.VMEM(square, F32), pltpu.VMEM((packed, 2 * channels), F32)]
+        scratch += [pltpu.VMEM((packed, 2 * channels), F32)]
     else:
         shapes += [jax.ShapeDtypeStruct(s, F32) for s in (square, slab, tile)]
     hidden, *rest = call(
@@ -486,9 +534,9 @@
         far = lax.ppermute(far_row, BOTH, beyond)
         shared = (cotangent, back_grad, weights, bias_tile, taps)
         inside = list(range(1, rows - 1))
-        inner, *sums = layer("layer_inside", inside, lines, None, *shared, None)
+        inner, *sums = layer("layer_inside", inside, lines, None, *shared, None, INSIDE_FRAMES)
         halo = (side, near, far)
-        outer, mine, other = layer("layer_edges", [0, rows - 1], lines, halo, *shared, sums)
+        outer, mine, other = layer("layer_edges", [0, rows - 1], lines, halo, *shared, sums, EDGE_FRAMES)
         made = []
 
         def output_of(parity):

time: 97.3 us -> 92.3 us (0.949)
  Pallas kernels: 24.5 us -> 20.7 us
  local copies, waits for them, and re-layouts: 2.93 us -> 0.06 us
  starting transfers between devices: 24.3 us -> 25.4 us
    pallas_call x2, Pallas kernels: 16 us -> 9.14 us  [layer(): call(kernel, name, tuple(shapes), 8 * (2 * 9 + taps) * channels * total *...]
    pallas_call x2, Pallas kernels: 4.22 us -> 7.33 us  [the longest x1 4.8 us: prepare(): call(kernel, 'prepare', (pltpu.HBM(cotangent.shape, BF16), jax.ShapeDtype...]
    unnamed x10 -> x8, local copies, waits for them, and re-layouts: 2.93 us -> 0.06 us
    ppermute x3, starting transfers between devices: 10.4 us -> 11.6 us  [sum_over_devices(): lax.ppermute(part, 'frame', [(i, i ^ bit) for i in range(owners)])]
    ppermute x3, waiting for transfers between devices: 5.46 us -> 6.48 us  [sum_over_devices(): lax.ppermute(part, 'frame', [(i, i ^ bit) for i in range(owners)])]
  transfers between devices with their start and end apart: 8 -> 8, of which waited for: 6 -> 6; matrix products, arithmetic and copies ran while one was open for 0% -> 0% of each run, Pallas kernels for 15% -> 16%
where the time goes in v1:
time: 92.3 us; the launch traced here: 92 us
  waiting for transfers between devices  45 us (49%)
  starting transfers between devices  25.4 us (28%)
  Pallas kernels  20.7 us (22%)
    all_to_all x1, waiting for transfers between devices, body(): lax.all_to_all(pack(frames, count), BOTH, split_axis=0, concat_axis=0, ti...  36.3 us
    ppermute x3, starting transfers between devices, sum_over_devices(): lax.ppermute(part, 'frame', [(i, i ^ bit) for i in range(owners)])  11.6 us
    pallas_call x2, Pallas kernels, layer(): call(kernel, name, tuple(shapes), 8 * (2 * 9 + taps) * channels * total *...  9.14 us
    all_to_all x1, starting transfers between devices, body(): lax.all_to_all(pack(frames, count), BOTH, split_axis=0, concat_axis=0, ti...  7.53 us
    ppermute x3, waiting for transfers between devices, sum_over_devices(): lax.ppermute(part, 'frame', [(i, i ^ bit) for i in range(owners)])  6.48 us
    pallas_call x1, Pallas kernels, prepare(): call(kernel, 'prepare', (pltpu.HBM(cotangent.shape, BF16), jax.ShapeDtype...  4.8 us
    ppermute x1, starting transfers between devices, sum_over_devices(): part = mine + lax.ppermute(other, BOTH, beside)  4.76 us
    pallas_call x2, Pallas kernels, temporal_output(): call(kernel, 'temporal_output', jax.ShapeDtypeStruct((count, 2, channels,...  3.33 us
  transfers between devices with their start and end apart: 8, of which 6 were waited for; matrix products, arithmetic and copies ran while one was open for 0% of the time, Pallas kernels for 16%

profile of v1, /device:TPU:0, one launch (start us, length us, event | category | flops | bytes accessed | tf_op | source)
XLA Modules:
  0.0 92.0 jit_solution(4261862445629738059)
XLA Ops:
  0.6 2.5 %pack.1 = bf16[16,2,8,32,128]{4,3,2,1,0:T(8,128)(2,1)} custom-call(bf16[2,32,128,128]{3,2,1,0:T(8,128)(2,1)} %images_ref.1), custom_call_target="tpu_custom_call" | custom-call | flops 1048576 | bytes 4194304 | tf_op jit(solution)/shard_map/pack/pallas_call | solution.py:75
  3.2 0.0 copy-start
  3.2 0.0 copy-start.1
  3.2 0.0 copy-start.2
  3.2 7.5 %all-to-all-start = ((bf16[16,2,8,32,128]{4,3,2,1,0:T(8,128)(2,1)}), bf16[16,2,8,32,128]{4,3,2,1,0:T(8,128)(2,1)S(1)}, u32[]{:S(2)}, u32[]{:S(2)}) async-start(bf16[16,2,8,32,128]{4,3,2,1,0:T(8,128)(2,1)} %pack.1), calls=%async_computation | async-start | bytes 4194304 | tf_op jit(solution)/shard_map/all_to_all | solution.py:526
  10.7 0.0 copy-done
  10.7 0.0 copy-done.1
  10.8 0.0 copy-done.2
  10.8 4.8 %prepare.1 = (bf16[16,64,1024]{2,1,0:T(8,128)(2,1)}, bf16[192,192]{1,0:T(8,128)(2,1)S(1)}, f32[64,128]{1,0:T(8,128)S(1)}) custom-call(bf16[16,64,1024]{2,1,0:T(8,128)(2,1)} %cot_ref.1, bf16[3,64,64]{2,1,0:T(8,128)(2,1)S(1)} %copy-done, bf16[9,64,64]{2,1,0:T(8,128)(2,1)S(1)} %copy-done.1, f32[1,64]{1,0:T(1,128)S(1)} %bitcast.10), custom_call_target="tpu_custom_call" | custom-call | flops 1610612736 | bytes 4407296 | tf_op jit(solution)/shard_map/prepare/pallas_call | solution.py:147
  15.6 36.3 %all-to-all-done = bf16[16,2,8,32,128]{4,3,2,1,0:T(8,128)(2,1)S(1)} async-done(((bf16[16,2,8,32,128]{4,3,2,1,0:T(8,128)(2,1)}), bf16[16,2,8,32,128]{4,3,2,1,0:T(8,128)(2,1)S(1)}, u32[]{:S(2)}, u32[]{:S(2)}) %all-to-all-start) | async-done | bytes 2097184 | tf_op jit(solution)/shard_map/all_to_all | solution.py:526
  51.8 0.0 copy-start.3
  51.9 0.8 collective-permute-start
  52.7 0.7 collective-permute-start.1
  53.4 0.0 copy-done.3
  53.4 6.5 %layer_inside.1 = (bf16[8,2,64,768]{3,2,1,0:T(8,128)(2,1)S(1)}, f32[192,192]{1,0:T(8,128)S(1)}, f32[3,64,64]{2,1,0:T(8,128)S(1)}, f32[64,128]{1,0:T(8,128)S(1)}) custom-call(bf16[8,2,2,8,32,128]{5,4,3,2,1,0:T(8,128)(2,1)S(1)} %bitcast.8, bf16[8,2,64,1024]{3,2,1,0:T(8,128)(2,1)} %bitcast.14, bf16[8,2,64,1024]{3,2,1,0:T(8,128)(2,1)S(1)} %bitcast.11, ...), custom_call_target="tpu_custom_call" | custom-call | flops 8455716864 | bytes 3604480 | tf_op jit(solution)/shard_map/layer_inside/pallas_call | solution.py:462
  60.0 0.0 collective-permute-done.refs_1_
  60.0 0.0 collective-permute-done.1.refs_2_
  60.0 2.6 %layer_edges.1 = (bf16[8,2,64,256]{3,2,1,0:T(8,128)(2,1)S(1)}, f32[200,128]{1,0:T(8,128)S(1)}, f32[200,128]{1,0:T(8,128)S(1)}) custom-call(s32[1]{0:T(128)} %bitcast.side_ref.refs_0_, bf16[8,2,2,32,128]{4,3,2,1,0:T(8,128)(2,1)S(1)} %collective-permute-done.refs_1_, bf16[8,2,2,32,128]{4,3,2,1,0:T(8,128)(2,1)S(1)} %collective-permute-done.1.refs_2_, ...), custom_call_target="tpu_custom_call" | custom-call | flops 2818572288 | bytes 1458176 | tf_op jit(solution)/shard_map/layer_edges/pallas_call | solution.py:462
  62.6 4.8 %collective-permute-start.2 = (f32[200,128]{1,0:T(8,128)S(1)}, f32[200,128]{1,0:T(8,128)S(1)}, u32[]{:S(2)}, u32[]{:S(2)}) collective-permute-start(f32[200,128]{1,0:T(8,128)S(1)} %get-tuple-element.32), channel_id=1, source_target_pairs={{0,1},{1,0},{2,3},{3,2},{4,5},{5,4},{6,7},{7,6},{8,9},{9,8},{10,11... | collective-permute-start | bytes 307208 | tf_op jit(solution)/shard_map/ppermute | solution.py:475
  67.4 0.9 %collective-permute-done.2 = f32[200,128]{1,0:T(8,128)S(1)} collective-permute-done((f32[200,128]{1,0:T(8,128)S(1)}, f32[200,128]{1,0:T(8,128)S(1)}, u32[]{:S(2)}, u32[]{:S(2)}) %collective-permute-start.2) | collective-permute-done | bytes 102432 | tf_op jit(solution)/shard_map/ppermute | solution.py:475
  68.3 4.5 %collective-permute-start.3 = (f32[200,128]{1,0:T(8,128)S(1)}, f32[200,128]{1,0:T(8,128)S(1)}, u32[]{:S(2)}, u32[]{:S(2)}) collective-permute-start(f32[200,128]{1,0:T(8,128)S(1)} %add.12), channel_id=1, source_target_pairs={{0,2},{2,0},{4,6},{6,4},{8,10},{10,8},{12,14},{14,12},{1,3},{3,1},... | collective-permute-start | bytes 307208 | tf_op jit(solution)/shard_map/ppermute | solution.py:478
  72.8 3.4 %collective-permute-done.3 = f32[200,128]{1,0:T(8,128)S(1)} collective-permute-done((f32[200,128]{1,0:T(8,128)S(1)}, f32[200,128]{1,0:T(8,128)S(1)}, u32[]{:S(2)}, u32[]{:S(2)}) %collective-permute-start.3) | collective-permute-done | bytes 102432 | tf_op jit(solution)/shard_map/ppermute | solution.py:478
  76.2 3.5 %collective-permute-start.4 = (f32[200,128]{1,0:T(8,128)S(1)}, f32[200,128]{1,0:T(8,128)S(1)}, u32[]{:S(2)}, u32[]{:S(2)}) collective-permute-start(f32[200,128]{1,0:T(8,128)S(1)} %add.13), channel_id=1, source_target_pairs={{0,4},{2,6},{4,0},{6,2},{8,12},{10,14},{12,8},{14,10},{1,5},{3,7},... | collective-permute-start | bytes 307208 | tf_op jit(solution)/shard_map/ppermute | solution.py:478
  79.8 1.7 %temporal_output.2.refs_3_ = bf16[8,2,64,1024]{3,2,1,0:T(8,128)(2,1)} custom-call(bf16[8,2,64,768]{3,2,1,0:T(8,128)(2,1)S(1)} %get-tuple-element.33.refs_0_, bf16[8,2,64,256]{3,2,1,0:T(8,128)(2,1)S(1)} %get-tuple-element.34.refs_1_, bf16[3,64,64]{2,1,0:T(8,128)(2,1)S(1)} %copy-done), custom_call_target="tpu_custom_call" | custom-call | flops 1207959552 | bytes 4194304 | tf_op jit(solution)/shard_map/temporal_output/pallas_call | solution.py:224
  81.4 1.0 %collective-permute-done.4 = f32[200,128]{1,0:T(8,128)S(1)} collective-permute-done((f32[200,128]{1,0:T(8,128)S(1)}, f32[200,128]{1,0:T(8,128)S(1)}, u32[]{:S(2)}, u32[]{:S(2)}) %collective-permute-start.4) | collective-permute-done | bytes 102432 | tf_op jit(solution)/shard_map/ppermute | solution.py:478
  82.5 3.5 %collective-permute-start.5 = (f32[200,128]{1,0:T(8,128)S(1)}, f32[200,128]{1,0:T(8,128)S(1)}, u32[]{:S(2)}, u32[]{:S(2)}) collective-permute-start(f32[200,128]{1,0:T(8,128)S(1)} %add.14), channel_id=1, source_target_pairs={{0,8},{2,10},{4,12},{6,14},{8,0},{10,2},{12,4},{14,6},{1,9},{3,11}... | collective-permute-start | bytes 307208 | tf_op jit(solution)/shard_map/ppermute | solution.py:478
  86.0 1.7 %temporal_output.3 = bf16[8,2,64,1024]{3,2,1,0:T(8,128)(2,1)} custom-call(bf16[8,2,64,768]{3,2,1,0:T(8,128)(2,1)S(1)} %get-tuple-element.33.refs_0_, bf16[8,2,64,256]{3,2,1,0:T(8,128)(2,1)S(1)} %get-tuple-element.34.refs_1_, bf16[3,64,64]{2,1,0:T(8,128)(2,1)S(1)} %copy-done, ...), custom_call_target="tpu_custom_call", output_to_operand_aliasing={{}: (3, {})} | custom-call | flops 1207959552 | bytes 4194304 | tf_op jit(solution)/shard_map/temporal_output/pallas_call | solution.py:224
  87.7 2.1 %collective-permute-done.5 = f32[200,128]{1,0:T(8,128)S(1)} collective-permute-done((f32[200,128]{1,0:T(8,128)S(1)}, f32[200,128]{1,0:T(8,128)S(1)}, u32[]{:S(2)}, u32[]{:S(2)}) %collective-permute-start.5) | collective-permute-done | bytes 102432 | tf_op jit(solution)/shard_map/ppermute | solution.py:478
  89.8 0.1 collective-permute-start.6
  89.8 1.3 %collective-permute-done.6.other_ref = f32[200,128]{1,0:T(8,128)S(1)} collective-permute-done((f32[200,128]{1,0:T(8,128)S(1)}, f32[200,128]{1,0:T(8,128)S(1)}, u32[]{:S(2)}, u32[]{:S(2)}) %collective-permute-start.6) | collective-permute-done | bytes 102432 | tf_op jit(solution)/shard_map/ppermute | solution.py:552
  91.1 0.9 unpack.1
  (5 shorter events, 0.1 us)
Async XLA Ops:
  3.2 7.6 %copy-start = (bf16[3,64,64]{2,1,0:T(8,128)(2,1)S(1)}, bf16[3,64,64]{2,1,0:T(8,128)(2,1)}, u32[]{:S(2)}) copy-start(bf16[3,64,64]{2,1,0:T(8,128)(2,1)} %refs_2_.3) | copy-start | bytes 73732
  3.2 7.6 %copy-start.1 = (bf16[9,64,64]{2,1,0:T(8,128)(2,1)S(1)}, bf16[9,64,64]{2,1,0:T(8,128)(2,1)}, u32[]{:S(2)}) copy-start(bf16[9,64,64]{2,1,0:T(8,128)(2,1)} %sw_ref.1) | copy-start | bytes 221188
  3.2 7.6 %copy-start.2 = (f32[64]{0:T(128)S(1)}, f32[64]{0:T(128)}, u32[]{:S(2)}) copy-start(f32[64]{0:T(128)} %param.7) | copy-start | bytes 772
  3.2 48.6 %all-to-all-start = ((bf16[16,2,8,32,128]{4,3,2,1,0:T(8,128)(2,1)}), bf16[16,2,8,32,128]{4,3,2,1,0:T(8,128)(2,1)S(1)}, u32[]{:S(2)}, u32[]{:S(2)}) async-start(bf16[16,2,8,32,128]{4,3,2,1,0:T(8,128)(2,1)} %pack.1), calls=%async_computation | async-start | bytes 4194304 | tf_op jit(solution)/shard_map/all_to_all | solution.py:526
  51.8 1.6 %copy-start.3 = (bf16[16,64,1024]{2,1,0:T(8,128)(2,1)S(1)}, bf16[16,64,1024]{2,1,0:T(8,128)(2,1)}, u32[]{:S(2)}) copy-start(bf16[16,64,1024]{2,1,0:T(8,128)(2,1)} %get-tuple-element.25) | copy-start | bytes 6291460
  51.9 8.1 %collective-permute-start = (bf16[8,2,2,32,128]{4,3,2,1,0:T(8,128)(2,1)S(1)}, bf16[8,2,2,32,128]{4,3,2,1,0:T(8,128)(2,1)S(1)}, u32[]{:S(2)}, u32[]{:S(2)}) collective-permute-start(bf16[8,2,2,32,128]{4,3,2,1,0:T(8,128)(2,1)S(1)} %get-tuple-element.23), channel_id=1, source_target_pairs={{0,1},{1,0},{2,3},{3,2},{4,5},{5,4},{6,7},{7,6},{8,9},{9,8},{10,11... | collective-permute-start | bytes 786440 | tf_op jit(solution)/shard_map/ppermute | solution.py:533
  52.7 7.3 %collective-permute-start.1 = (bf16[8,2,2,32,128]{4,3,2,1,0:T(8,128)(2,1)S(1)}, bf16[8,2,2,32,128]{4,3,2,1,0:T(8,128)(2,1)S(1)}, u32[]{:S(2)}, u32[]{:S(2)}) collective-permute-start(bf16[8,2,2,32,128]{4,3,2,1,0:T(8,128)(2,1)S(1)} %get-tuple-element.24), channel_id=1, source_target_pairs={{2,1},{4,3},{6,5},{8,7},{10,9},{12,11},{14,13},{1,2},{3,4},{5,6},{... | collective-permute-start | bytes 786440 | tf_op jit(solution)/shard_map/ppermute | solution.py:534
  62.6 5.7 %collective-permute-start.2 = (f32[200,128]{1,0:T(8,128)S(1)}, f32[200,128]{1,0:T(8,128)S(1)}, u32[]{:S(2)}, u32[]{:S(2)}) collective-permute-start(f32[200,128]{1,0:T(8,128)S(1)} %get-tuple-element.32), channel_id=1, source_target_pairs={{0,1},{1,0},{2,3},{3,2},{4,5},{5,4},{6,7},{7,6},{8,9},{9,8},{10,11... | collective-permute-start | bytes 307208 | tf_op jit(solution)/shard_map/ppermute | solution.py:475
  68.3 7.9 %collective-permute-start.3 = (f32[200,128]{1,0:T(8,128)S(1)}, f32[200,128]{1,0:T(8,128)S(1)}, u32[]{:S(2)}, u32[]{:S(2)}) collective-permute-start(f32[200,128]{1,0:T(8,128)S(1)} %add.12), channel_id=1, source_target_pairs={{0,2},{2,0},{4,6},{6,4},{8,10},{10,8},{12,14},{14,12},{1,3},{3,1},... | collective-permute-start | bytes 307208 | tf_op jit(solution)/shard_map/ppermute | solution.py:478
  76.2 6.2 %collective-permute-start.4 = (f32[200,128]{1,0:T(8,128)S(1)}, f32[200,128]{1,0:T(8,128)S(1)}, u32[]{:S(2)}, u32[]{:S(2)}) collective-permute-start(f32[200,128]{1,0:T(8,128)S(1)} %add.13), channel_id=1, source_target_pairs={{0,4},{2,6},{4,0},{6,2},{8,12},{10,14},{12,8},{14,10},{1,5},{3,7},... | collective-permute-start | bytes 307208 | tf_op jit(solution)/shard_map/ppermute | solution.py:478
  82.5 7.3 %collective-permute-start.5 = (f32[200,128]{1,0:T(8,128)S(1)}, f32[200,128]{1,0:T(8,128)S(1)}, u32[]{:S(2)}, u32[]{:S(2)}) collective-permute-start(f32[200,128]{1,0:T(8,128)S(1)} %add.14), channel_id=1, source_target_pairs={{0,8},{2,10},{4,12},{6,14},{8,0},{10,2},{12,4},{14,6},{1,9},{3,11}... | collective-permute-start | bytes 307208 | tf_op jit(solution)/shard_map/ppermute | solution.py:478
  89.8 1.4 %collective-permute-start.6 = (f32[200,128]{1,0:T(8,128)S(1)}, f32[200,128]{1,0:T(8,128)S(1)}, u32[]{:S(2)}, u32[]{:S(2)}) collective-permute-start(f32[200,128]{1,0:T(8,128)S(1)} %add.15.mine_ref), channel_id=1, source_target_pairs={{0,1},{1,0},{2,3},{3,2},{4,5},{5,4},{6,7},{7,6},{8,9},{9,8},{10,11... | collective-permute-start | bytes 307208 | tf_op jit(solution)/shard_map/ppermute | solution.py:552

commit v2 on v1

--- a/solution.py
+++ b/solution.py
@@ -473,12 +473,15 @@
 
 def sum_over_devices(mine, other, owners, beside, beneath):
     part = mine + lax.ppermute(other, BOTH, beside)
-    bit = 1
-    while bit < owners:
-        part = part + lax.ppermute(part, "frame", [(i, i ^ bit) for i in range(owners)])
-        if bit > 1 and beneath:
+    bits = [1 << n for n in range(owners.bit_length() - 1)]
+    orders = (bits, bits[-1:] + bits[:-1])
+    for stage in range(len(bits)):
+        pairs = [
+            (2 * f + c, 2 * (f ^ orders[c][stage]) + c) for f in range(owners) for c in range(2)
+        ]
+        part = part + lax.ppermute(part, BOTH, pairs)
+        if stage > 0 and beneath:
             part = beneath.pop(0)(part)
-        bit *= 2
     return part
 
 

time: 92.3 us -> 91.8 us (level)
  no operation moved by 1% of the time
where the time goes in v2:
time: 91.8 us; the launch traced here: 91.5 us
  waiting for transfers between devices  44.2 us (48%)
  starting transfers between devices  25.7 us (28%)
  Pallas kernels  20.7 us (23%)
    all_to_all x1, waiting for transfers between devices, body(): lax.all_to_all(pack(frames, count), BOTH, split_axis=0, concat_axis=0, ti...  36.3 us
    ppermute x3, starting transfers between devices, sum_over_devices(): part = part + lax.ppermute(part, BOTH, pairs)  11.9 us
    pallas_call x2, Pallas kernels, layer(): call(kernel, name, tuple(shapes), 8 * (2 * 9 + taps) * channels * total *...  9.14 us
    all_to_all x1, starting transfers between devices, body(): lax.all_to_all(pack(frames, count), BOTH, split_axis=0, concat_axis=0, ti...  7.53 us
    ppermute x3, waiting for transfers between devices, sum_over_devices(): part = part + lax.ppermute(part, BOTH, pairs)  5.65 us
    pallas_call x1, Pallas kernels, prepare(): call(kernel, 'prepare', (pltpu.HBM(cotangent.shape, BF16), jax.ShapeDtype...  4.8 us
    ppermute x1, starting transfers between devices, sum_over_devices(): part = mine + lax.ppermute(other, BOTH, beside)  4.76 us
    pallas_call x2, Pallas kernels, temporal_output(): call(kernel, 'temporal_output', jax.ShapeDtypeStruct((count, 2, channels,...  3.37 us
  transfers between devices with their start and end apart: 8, of which 6 were waited for; matrix products, arithmetic and copies ran while one was open for 0% of the time, Pallas kernels for 16%

profile of v2, /device:TPU:0, one launch (start us, length us, event | category | flops | bytes accessed | tf_op | source)
XLA Modules:
  0.0 91.5 jit_solution(11080936596866194304)
XLA Ops:
  0.6 2.5 %pack.1 = bf16[16,2,8,32,128]{4,3,2,1,0:T(8,128)(2,1)} custom-call(bf16[2,32,128,128]{3,2,1,0:T(8,128)(2,1)} %images_ref.1), custom_call_target="tpu_custom_call" | custom-call | flops 1048576 | bytes 4194304 | tf_op jit(solution)/shard_map/pack/pallas_call | solution.py:75
  3.2 0.0 copy-start
  3.2 0.0 copy-start.1
  3.2 0.0 copy-start.2
  3.2 7.5 %all-to-all-start = ((bf16[16,2,8,32,128]{4,3,2,1,0:T(8,128)(2,1)}), bf16[16,2,8,32,128]{4,3,2,1,0:T(8,128)(2,1)S(1)}, u32[]{:S(2)}, u32[]{:S(2)}) async-start(bf16[16,2,8,32,128]{4,3,2,1,0:T(8,128)(2,1)} %pack.1), calls=%async_computation | async-start | bytes 4194304 | tf_op jit(solution)/shard_map/all_to_all | solution.py:529
  10.7 0.0 copy-done
  10.7 0.0 copy-done.1
  10.8 0.0 copy-done.2
  10.8 4.8 %prepare.1 = (bf16[16,64,1024]{2,1,0:T(8,128)(2,1)}, bf16[192,192]{1,0:T(8,128)(2,1)S(1)}, f32[64,128]{1,0:T(8,128)S(1)}) custom-call(bf16[16,64,1024]{2,1,0:T(8,128)(2,1)} %cot_ref.1, bf16[3,64,64]{2,1,0:T(8,128)(2,1)S(1)} %copy-done, bf16[9,64,64]{2,1,0:T(8,128)(2,1)S(1)} %copy-done.1, f32[1,64]{1,0:T(1,128)S(1)} %bitcast.10), custom_call_target="tpu_custom_call" | custom-call | flops 1610612736 | bytes 4407296 | tf_op jit(solution)/shard_map/prepare/pallas_call | solution.py:147
  15.6 36.3 %all-to-all-done = bf16[16,2,8,32,128]{4,3,2,1,0:T(8,128)(2,1)S(1)} async-done(((bf16[16,2,8,32,128]{4,3,2,1,0:T(8,128)(2,1)}), bf16[16,2,8,32,128]{4,3,2,1,0:T(8,128)(2,1)S(1)}, u32[]{:S(2)}, u32[]{:S(2)}) %all-to-all-start) | async-done | bytes 2097184 | tf_op jit(solution)/shard_map/all_to_all | solution.py:529
  51.8 0.0 copy-start.3
  51.9 0.8 collective-permute-start
  52.7 0.7 collective-permute-start.1
  53.4 0.0 copy-done.3
  53.4 6.5 %layer_inside.1 = (bf16[8,2,64,768]{3,2,1,0:T(8,128)(2,1)S(1)}, f32[192,192]{1,0:T(8,128)S(1)}, f32[3,64,64]{2,1,0:T(8,128)S(1)}, f32[64,128]{1,0:T(8,128)S(1)}) custom-call(bf16[8,2,2,8,32,128]{5,4,3,2,1,0:T(8,128)(2,1)S(1)} %bitcast.8, bf16[8,2,64,1024]{3,2,1,0:T(8,128)(2,1)} %bitcast.14, bf16[8,2,64,1024]{3,2,1,0:T(8,128)(2,1)S(1)} %bitcast.11, ...), custom_call_target="tpu_custom_call" | custom-call | flops 8455716864 | bytes 3604480 | tf_op jit(solution)/shard_map/layer_inside/pallas_call | solution.py:462
  60.0 0.0 collective-permute-done.refs_1_
  60.0 0.0 collective-permute-done.1.refs_2_
  60.0 2.6 %layer_edges.1 = (bf16[8,2,64,256]{3,2,1,0:T(8,128)(2,1)S(1)}, f32[200,128]{1,0:T(8,128)S(1)}, f32[200,128]{1,0:T(8,128)S(1)}) custom-call(s32[1]{0:T(128)} %bitcast.side_ref.refs_0_, bf16[8,2,2,32,128]{4,3,2,1,0:T(8,128)(2,1)S(1)} %collective-permute-done.refs_1_, bf16[8,2,2,32,128]{4,3,2,1,0:T(8,128)(2,1)S(1)} %collective-permute-done.1.refs_2_, ...), custom_call_target="tpu_custom_call" | custom-call | flops 2818572288 | bytes 1458176 | tf_op jit(solution)/shard_map/layer_edges/pallas_call | solution.py:462
  62.6 4.8 %collective-permute-start.2 = (f32[200,128]{1,0:T(8,128)S(1)}, f32[200,128]{1,0:T(8,128)S(1)}, u32[]{:S(2)}, u32[]{:S(2)}) collective-permute-start(f32[200,128]{1,0:T(8,128)S(1)} %get-tuple-element.32), channel_id=1, source_target_pairs={{0,1},{1,0},{2,3},{3,2},{4,5},{5,4},{6,7},{7,6},{8,9},{9,8},{10,11... | collective-permute-start | bytes 307208 | tf_op jit(solution)/shard_map/ppermute | solution.py:475
  67.4 0.9 %collective-permute-done.2 = f32[200,128]{1,0:T(8,128)S(1)} collective-permute-done((f32[200,128]{1,0:T(8,128)S(1)}, f32[200,128]{1,0:T(8,128)S(1)}, u32[]{:S(2)}, u32[]{:S(2)}) %collective-permute-start.2) | collective-permute-done | bytes 102432 | tf_op jit(solution)/shard_map/ppermute | solution.py:475
  68.3 4.5 %collective-permute-start.3 = (f32[200,128]{1,0:T(8,128)S(1)}, f32[200,128]{1,0:T(8,128)S(1)}, u32[]{:S(2)}, u32[]{:S(2)}) collective-permute-start(f32[200,128]{1,0:T(8,128)S(1)} %add.12), channel_id=1, source_target_pairs={{0,2},{1,9},{2,0},{3,11},{4,6},{5,13},{6,4},{7,15},{8,10},{9,1},{1... | collective-permute-start | bytes 307208 | tf_op jit(solution)/shard_map/ppermute | solution.py:482
  72.8 2.6 %collective-permute-done.3 = f32[200,128]{1,0:T(8,128)S(1)} collective-permute-done((f32[200,128]{1,0:T(8,128)S(1)}, f32[200,128]{1,0:T(8,128)S(1)}, u32[]{:S(2)}, u32[]{:S(2)}) %collective-permute-start.3) | collective-permute-done | bytes 102432 | tf_op jit(solution)/shard_map/ppermute | solution.py:482
  75.5 3.8 %collective-permute-start.4 = (f32[200,128]{1,0:T(8,128)S(1)}, f32[200,128]{1,0:T(8,128)S(1)}, u32[]{:S(2)}, u32[]{:S(2)}) collective-permute-start(f32[200,128]{1,0:T(8,128)S(1)} %add.13), channel_id=1, source_target_pairs={{0,4},{1,3},{2,6},{3,1},{4,0},{5,7},{6,2},{7,5},{8,12},{9,11},{10,... | collective-permute-start | bytes 307208 | tf_op jit(solution)/shard_map/ppermute | solution.py:482
  79.2 1.7 %temporal_output.2.refs_3_ = bf16[8,2,64,1024]{3,2,1,0:T(8,128)(2,1)} custom-call(bf16[8,2,64,768]{3,2,1,0:T(8,128)(2,1)S(1)} %get-tuple-element.33.refs_0_, bf16[8,2,64,256]{3,2,1,0:T(8,128)(2,1)S(1)} %get-tuple-element.34.refs_1_, bf16[3,64,64]{2,1,0:T(8,128)(2,1)S(1)} %copy-done), custom_call_target="tpu_custom_call" | custom-call | flops 1207959552 | bytes 4194304 | tf_op jit(solution)/shard_map/temporal_output/pallas_call | solution.py:224
  80.9 1.0 %collective-permute-done.4 = f32[200,128]{1,0:T(8,128)S(1)} collective-permute-done((f32[200,128]{1,0:T(8,128)S(1)}, f32[200,128]{1,0:T(8,128)S(1)}, u32[]{:S(2)}, u32[]{:S(2)}) %collective-permute-start.4) | collective-permute-done | bytes 102432 | tf_op jit(solution)/shard_map/ppermute | solution.py:482
  81.9 3.6 %collective-permute-start.5 = (f32[200,128]{1,0:T(8,128)S(1)}, f32[200,128]{1,0:T(8,128)S(1)}, u32[]{:S(2)}, u32[]{:S(2)}) collective-permute-start(f32[200,128]{1,0:T(8,128)S(1)} %add.14), channel_id=1, source_target_pairs={{0,8},{1,5},{2,10},{3,7},{4,12},{5,1},{6,14},{7,3},{8,0},{9,13},{1... | collective-permute-start | bytes 307208 | tf_op jit(solution)/shard_map/ppermute | solution.py:482
  85.5 1.7 %temporal_output.3 = bf16[8,2,64,1024]{3,2,1,0:T(8,128)(2,1)} custom-call(bf16[8,2,64,768]{3,2,1,0:T(8,128)(2,1)S(1)} %get-tuple-element.33.refs_0_, bf16[8,2,64,256]{3,2,1,0:T(8,128)(2,1)S(1)} %get-tuple-element.34.refs_1_, bf16[3,64,64]{2,1,0:T(8,128)(2,1)S(1)} %copy-done, ...), custom_call_target="tpu_custom_call", output_to_operand_aliasing={{}: (3, {})} | custom-call | flops 1207959552 | bytes 4194304 | tf_op jit(solution)/shard_map/temporal_output/pallas_call | solution.py:224
  87.2 2.1 %collective-permute-done.5 = f32[200,128]{1,0:T(8,128)S(1)} collective-permute-done((f32[200,128]{1,0:T(8,128)S(1)}, f32[200,128]{1,0:T(8,128)S(1)}, u32[]{:S(2)}, u32[]{:S(2)}) %collective-permute-start.5) | collective-permute-done | bytes 102432 | tf_op jit(solution)/shard_map/ppermute | solution.py:482
  89.3 0.1 collective-permute-start.6
  89.4 1.3 %collective-permute-done.6.other_ref = f32[200,128]{1,0:T(8,128)S(1)} collective-permute-done((f32[200,128]{1,0:T(8,128)S(1)}, f32[200,128]{1,0:T(8,128)S(1)}, u32[]{:S(2)}, u32[]{:S(2)}) %collective-permute-start.6) | collective-permute-done | bytes 102432 | tf_op jit(solution)/shard_map/ppermute | solution.py:555
  90.6 0.9 unpack.1
  (5 shorter events, 0.1 us)
Async XLA Ops:
  3.2 7.6 %copy-start = (bf16[3,64,64]{2,1,0:T(8,128)(2,1)S(1)}, bf16[3,64,64]{2,1,0:T(8,128)(2,1)}, u32[]{:S(2)}) copy-start(bf16[3,64,64]{2,1,0:T(8,128)(2,1)} %refs_2_.3) | copy-start | bytes 73732
  3.2 7.6 %copy-start.1 = (bf16[9,64,64]{2,1,0:T(8,128)(2,1)S(1)}, bf16[9,64,64]{2,1,0:T(8,128)(2,1)}, u32[]{:S(2)}) copy-start(bf16[9,64,64]{2,1,0:T(8,128)(2,1)} %sw_ref.1) | copy-start | bytes 221188
  3.2 7.6 %copy-start.2 = (f32[64]{0:T(128)S(1)}, f32[64]{0:T(128)}, u32[]{:S(2)}) copy-start(f32[64]{0:T(128)} %param.7) | copy-start | bytes 772
  3.2 48.6 %all-to-all-start = ((bf16[16,2,8,32,128]{4,3,2,1,0:T(8,128)(2,1)}), bf16[16,2,8,32,128]{4,3,2,1,0:T(8,128)(2,1)S(1)}, u32[]{:S(2)}, u32[]{:S(2)}) async-start(bf16[16,2,8,32,128]{4,3,2,1,0:T(8,128)(2,1)} %pack.1), calls=%async_computation | async-start | bytes 4194304 | tf_op jit(solution)/shard_map/all_to_all | solution.py:529
  51.8 1.6 %copy-start.3 = (bf16[16,64,1024]{2,1,0:T(8,128)(2,1)S(1)}, bf16[16,64,1024]{2,1,0:T(8,128)(2,1)}, u32[]{:S(2)}) copy-start(bf16[16,64,1024]{2,1,0:T(8,128)(2,1)} %get-tuple-element.25) | copy-start | bytes 6291460
  51.9 8.1 %collective-permute-start = (bf16[8,2,2,32,128]{4,3,2,1,0:T(8,128)(2,1)S(1)}, bf16[8,2,2,32,128]{4,3,2,1,0:T(8,128)(2,1)S(1)}, u32[]{:S(2)}, u32[]{:S(2)}) collective-permute-start(bf16[8,2,2,32,128]{4,3,2,1,0:T(8,128)(2,1)S(1)} %get-tuple-element.23), channel_id=1, source_target_pairs={{0,1},{1,0},{2,3},{3,2},{4,5},{5,4},{6,7},{7,6},{8,9},{9,8},{10,11... | collective-permute-start | bytes 786440 | tf_op jit(solution)/shard_map/ppermute | solution.py:536
  52.7 7.3 %collective-permute-start.1 = (bf16[8,2,2,32,128]{4,3,2,1,0:T(8,128)(2,1)S(1)}, bf16[8,2,2,32,128]{4,3,2,1,0:T(8,128)(2,1)S(1)}, u32[]{:S(2)}, u32[]{:S(2)}) collective-permute-start(bf16[8,2,2,32,128]{4,3,2,1,0:T(8,128)(2,1)S(1)} %get-tuple-element.24), channel_id=1, source_target_pairs={{2,1},{4,3},{6,5},{8,7},{10,9},{12,11},{14,13},{1,2},{3,4},{5,6},{... | collective-permute-start | bytes 786440 | tf_op jit(solution)/shard_map/ppermute | solution.py:537
  62.6 5.7 %collective-permute-start.2 = (f32[200,128]{1,0:T(8,128)S(1)}, f32[200,128]{1,0:T(8,128)S(1)}, u32[]{:S(2)}, u32[]{:S(2)}) collective-permute-start(f32[200,128]{1,0:T(8,128)S(1)} %get-tuple-element.32), channel_id=1, source_target_pairs={{0,1},{1,0},{2,3},{3,2},{4,5},{5,4},{6,7},{7,6},{8,9},{9,8},{10,11... | collective-permute-start | bytes 307208 | tf_op jit(solution)/shard_map/ppermute | solution.py:475
  68.3 7.1 %collective-permute-start.3 = (f32[200,128]{1,0:T(8,128)S(1)}, f32[200,128]{1,0:T(8,128)S(1)}, u32[]{:S(2)}, u32[]{:S(2)}) collective-permute-start(f32[200,128]{1,0:T(8,128)S(1)} %add.12), channel_id=1, source_target_pairs={{0,2},{1,9},{2,0},{3,11},{4,6},{5,13},{6,4},{7,15},{8,10},{9,1},{1... | collective-permute-start | bytes 307208 | tf_op jit(solution)/shard_map/ppermute | solution.py:482
  75.5 6.4 %collective-permute-start.4 = (f32[200,128]{1,0:T(8,128)S(1)}, f32[200,128]{1,0:T(8,128)S(1)}, u32[]{:S(2)}, u32[]{:S(2)}) collective-permute-start(f32[200,128]{1,0:T(8,128)S(1)} %add.13), channel_id=1, source_target_pairs={{0,4},{1,3},{2,6},{3,1},{4,0},{5,7},{6,2},{7,5},{8,12},{9,11},{10,... | collective-permute-start | bytes 307208 | tf_op jit(solution)/shard_map/ppermute | solution.py:482
  81.9 7.4 %collective-permute-start.5 = (f32[200,128]{1,0:T(8,128)S(1)}, f32[200,128]{1,0:T(8,128)S(1)}, u32[]{:S(2)}, u32[]{:S(2)}) collective-permute-start(f32[200,128]{1,0:T(8,128)S(1)} %add.14), channel_id=1, source_target_pairs={{0,8},{1,5},{2,10},{3,7},{4,12},{5,1},{6,14},{7,3},{8,0},{9,13},{1... | collective-permute-start | bytes 307208 | tf_op jit(solution)/shard_map/ppermute | solution.py:482
  89.3 1.4 %collective-permute-start.6 = (f32[200,128]{1,0:T(8,128)S(1)}, f32[200,128]{1,0:T(8,128)S(1)}, u32[]{:S(2)}, u32[]{:S(2)}) collective-permute-start(f32[200,128]{1,0:T(8,128)S(1)} %add.15.mine_ref), channel_id=1, source_target_pairs={{0,1},{1,0},{2,3},{3,2},{4,5},{5,4},{6,7},{7,6},{8,9},{9,8},{10,11... | collective-permute-start | bytes 307208 | tf_op jit(solution)/shard_map/ppermute | solution.py:555

commit v3 on v2

--- a/solution.py
+++ b/solution.py
@@ -355,9 +355,14 @@
                         rounded = (back * slope).astype(BF16)
                         grad = rounded.astype(F32)
                         bias_sum = grad if bias_sum is None else bias_sum + grad
-                        gp_s[0:channels, place] = shifted(grad, -1).astype(BF16)
+                        nothing = jnp.zeros_like(rounded)
+                        gp_s[0:channels, place] = jnp.where(
+                            last, nothing, pltpu.roll(rounded, cols - 1, 1)
+                        )
                         gp_s[channels : 2 * channels, place] = rounded
-                        gp_s[2 * channels :, place] = shifted(grad, 1).astype(BF16)
+                        gp_s[2 * channels :, place] = jnp.where(
+                            first, nothing, pltpu.roll(rounded, 1, 1)
+                        )
             gb_s[...] += bias_sum
             whole = jnp.concatenate(
                 [
@@ -474,7 +479,7 @@
 def sum_over_devices(mine, other, owners, beside, beneath):
     part = mine + lax.ppermute(other, BOTH, beside)
     bits = [1 << n for n in range(owners.bit_length() - 1)]
-    orders = (bits, bits[-1:] + bits[:-1])
+    orders = (bits, bits[1:] + bits[:1])
     for stage in range(len(bits)):
         pairs = [
             (2 * f + c, 2 * (f ^ orders[c][stage]) + c) for f in range(owners) for c in range(2)

time: 91.8 us -> 90.7 us (0.988)
  no operation moved by 1% of the time
where the time goes in v3:
time: 90.7 us; the launch traced here: 90.4 us
  waiting for transfers between devices  43.6 us (48%)
  starting transfers between devices  25.8 us (28%)
  Pallas kernels  20.1 us (22%)
    all_to_all x1, waiting for transfers between devices, body(): lax.all_to_all(pack(frames, count), BOTH, split_axis=0, concat_axis=0, ti...  36.3 us
    ppermute x3, starting transfers between devices, sum_over_devices(): part = part + lax.ppermute(part, BOTH, pairs)  11.9 us
    pallas_call x2, Pallas kernels, layer(): call(kernel, name, tuple(shapes), 8 * (2 * 9 + taps) * channels * total *...  8.5 us
    all_to_all x1, starting transfers between devices, body(): lax.all_to_all(pack(frames, count), BOTH, split_axis=0, concat_axis=0, ti...  7.53 us
    ppermute x3, waiting for transfers between devices, sum_over_devices(): part = part + lax.ppermute(part, BOTH, pairs)  5.11 us
    pallas_call x1, Pallas kernels, prepare(): call(kernel, 'prepare', (pltpu.HBM(cotangent.shape, BF16), jax.ShapeDtype...  4.8 us
    ppermute x1, starting transfers between devices, sum_over_devices(): part = mine + lax.ppermute(other, BOTH, beside)  4.76 us
    pallas_call x2, Pallas kernels, temporal_output(): call(kernel, 'temporal_output', jax.ShapeDtypeStruct((count, 2, channels,...  3.35 us
  transfers between devices with their start and end apart: 8, of which 6 were waited for; matrix products, arithmetic and copies ran while one was open for 0% of the time, Pallas kernels for 16%

profile of v3, /device:TPU:0, one launch (start us, length us, event | category | flops | bytes accessed | tf_op | source)
XLA Modules:
  0.0 90.4 jit_solution(5602500154242083227)
XLA Ops:
  0.6 2.5 %pack.1 = bf16[16,2,8,32,128]{4,3,2,1,0:T(8,128)(2,1)} custom-call(bf16[2,32,128,128]{3,2,1,0:T(8,128)(2,1)} %images_ref.1), custom_call_target="tpu_custom_call" | custom-call | flops 1048576 | bytes 4194304 | tf_op jit(solution)/shard_map/pack/pallas_call | solution.py:75
  3.2 0.0 copy-start
  3.2 0.0 copy-start.1
  3.2 0.0 copy-start.2
  3.2 7.5 %all-to-all-start = ((bf16[16,2,8,32,128]{4,3,2,1,0:T(8,128)(2,1)}), bf16[16,2,8,32,128]{4,3,2,1,0:T(8,128)(2,1)S(1)}, u32[]{:S(2)}, u32[]{:S(2)}) async-start(bf16[16,2,8,32,128]{4,3,2,1,0:T(8,128)(2,1)} %pack.1), calls=%async_computation | async-start | bytes 4194304 | tf_op jit(solution)/shard_map/all_to_all | solution.py:534
  10.7 0.0 copy-done
  10.7 0.0 copy-done.1
  10.8 0.0 copy-done.2
  10.8 4.8 %prepare.1 = (bf16[16,64,1024]{2,1,0:T(8,128)(2,1)}, bf16[192,192]{1,0:T(8,128)(2,1)S(1)}, f32[64,128]{1,0:T(8,128)S(1)}) custom-call(bf16[16,64,1024]{2,1,0:T(8,128)(2,1)} %cot_ref.1, bf16[3,64,64]{2,1,0:T(8,128)(2,1)S(1)} %copy-done, bf16[9,64,64]{2,1,0:T(8,128)(2,1)S(1)} %copy-done.1, f32[1,64]{1,0:T(1,128)S(1)} %bitcast.10), custom_call_target="tpu_custom_call" | custom-call | flops 1610612736 | bytes 4407296 | tf_op jit(solution)/shard_map/prepare/pallas_call | solution.py:147
  15.6 36.3 %all-to-all-done = bf16[16,2,8,32,128]{4,3,2,1,0:T(8,128)(2,1)S(1)} async-done(((bf16[16,2,8,32,128]{4,3,2,1,0:T(8,128)(2,1)}), bf16[16,2,8,32,128]{4,3,2,1,0:T(8,128)(2,1)S(1)}, u32[]{:S(2)}, u32[]{:S(2)}) %all-to-all-start) | async-done | bytes 2097184 | tf_op jit(solution)/shard_map/all_to_all | solution.py:534
  51.8 0.0 copy-start.3
  51.9 0.8 collective-permute-start
  52.7 0.7 collective-permute-start.1
  53.4 0.0 copy-done.3
  53.4 5.9 %layer_inside.1 = (bf16[8,2,64,768]{3,2,1,0:T(8,128)(2,1)S(1)}, f32[192,192]{1,0:T(8,128)S(1)}, f32[3,64,64]{2,1,0:T(8,128)S(1)}, f32[64,128]{1,0:T(8,128)S(1)}) custom-call(bf16[8,2,2,8,32,128]{5,4,3,2,1,0:T(8,128)(2,1)S(1)} %bitcast.8, bf16[8,2,64,1024]{3,2,1,0:T(8,128)(2,1)} %bitcast.14, bf16[8,2,64,1024]{3,2,1,0:T(8,128)(2,1)S(1)} %bitcast.11, ...), custom_call_target="tpu_custom_call" | custom-call | flops 8455716864 | bytes 3604480 | tf_op jit(solution)/shard_map/layer_inside/pallas_call | solution.py:467
  59.3 0.0 collective-permute-done.refs_1_
  59.4 0.0 collective-permute-done.1.refs_2_
  59.4 2.6 %layer_edges.1 = (bf16[8,2,64,256]{3,2,1,0:T(8,128)(2,1)S(1)}, f32[200,128]{1,0:T(8,128)S(1)}, f32[200,128]{1,0:T(8,128)S(1)}) custom-call(s32[1]{0:T(128)} %bitcast.side_ref.refs_0_, bf16[8,2,2,32,128]{4,3,2,1,0:T(8,128)(2,1)S(1)} %collective-permute-done.refs_1_, bf16[8,2,2,32,128]{4,3,2,1,0:T(8,128)(2,1)S(1)} %collective-permute-done.1.refs_2_, ...), custom_call_target="tpu_custom_call" | custom-call | flops 2818572288 | bytes 1458176 | tf_op jit(solution)/shard_map/layer_edges/pallas_call | solution.py:467
  62.0 4.8 %collective-permute-start.2 = (f32[200,128]{1,0:T(8,128)S(1)}, f32[200,128]{1,0:T(8,128)S(1)}, u32[]{:S(2)}, u32[]{:S(2)}) collective-permute-start(f32[200,128]{1,0:T(8,128)S(1)} %get-tuple-element.32), channel_id=1, source_target_pairs={{0,1},{1,0},{2,3},{3,2},{4,5},{5,4},{6,7},{7,6},{8,9},{9,8},{10,11... | collective-permute-start | bytes 307208 | tf_op jit(solution)/shard_map/ppermute | solution.py:480
  66.7 0.9 %collective-permute-done.2 = f32[200,128]{1,0:T(8,128)S(1)} collective-permute-done((f32[200,128]{1,0:T(8,128)S(1)}, f32[200,128]{1,0:T(8,128)S(1)}, u32[]{:S(2)}, u32[]{:S(2)}) %collective-permute-start.2) | collective-permute-done | bytes 102432 | tf_op jit(solution)/shard_map/ppermute | solution.py:480
  67.7 4.5 %collective-permute-start.3 = (f32[200,128]{1,0:T(8,128)S(1)}, f32[200,128]{1,0:T(8,128)S(1)}, u32[]{:S(2)}, u32[]{:S(2)}) collective-permute-start(f32[200,128]{1,0:T(8,128)S(1)} %add.12), channel_id=1, source_target_pairs={{0,2},{1,5},{2,0},{3,7},{4,6},{5,1},{6,4},{7,3},{8,10},{9,13},{10,... | collective-permute-start | bytes 307208 | tf_op jit(solution)/shard_map/ppermute | solution.py:487
  72.2 2.6 %collective-permute-done.3 = f32[200,128]{1,0:T(8,128)S(1)} collective-permute-done((f32[200,128]{1,0:T(8,128)S(1)}, f32[200,128]{1,0:T(8,128)S(1)}, u32[]{:S(2)}, u32[]{:S(2)}) %collective-permute-start.3) | collective-permute-done | bytes 102432 | tf_op jit(solution)/shard_map/ppermute | solution.py:487
  74.8 4.4 %collective-permute-start.4 = (f32[200,128]{1,0:T(8,128)S(1)}, f32[200,128]{1,0:T(8,128)S(1)}, u32[]{:S(2)}, u32[]{:S(2)}) collective-permute-start(f32[200,128]{1,0:T(8,128)S(1)} %add.13), channel_id=1, source_target_pairs={{0,4},{1,9},{2,6},{3,11},{4,0},{5,13},{6,2},{7,15},{8,12},{9,1},{1... | collective-permute-start | bytes 307208 | tf_op jit(solution)/shard_map/ppermute | solution.py:487
  79.2 1.7 %temporal_output.2.refs_3_ = bf16[8,2,64,1024]{3,2,1,0:T(8,128)(2,1)} custom-call(bf16[8,2,64,768]{3,2,1,0:T(8,128)(2,1)S(1)} %get-tuple-element.33.refs_0_, bf16[8,2,64,256]{3,2,1,0:T(8,128)(2,1)S(1)} %get-tuple-element.34.refs_1_, bf16[3,64,64]{2,1,0:T(8,128)(2,1)S(1)} %copy-done), custom_call_target="tpu_custom_call" | custom-call | flops 1207959552 | bytes 4194304 | tf_op jit(solution)/shard_map/temporal_output/pallas_call | solution.py:224
  80.9 1.5 %collective-permute-done.4 = f32[200,128]{1,0:T(8,128)S(1)} collective-permute-done((f32[200,128]{1,0:T(8,128)S(1)}, f32[200,128]{1,0:T(8,128)S(1)}, u32[]{:S(2)}, u32[]{:S(2)}) %collective-permute-start.4) | collective-permute-done | bytes 102432 | tf_op jit(solution)/shard_map/ppermute | solution.py:487
  82.4 3.1 %collective-permute-start.5 = (f32[200,128]{1,0:T(8,128)S(1)}, f32[200,128]{1,0:T(8,128)S(1)}, u32[]{:S(2)}, u32[]{:S(2)}) collective-permute-start(f32[200,128]{1,0:T(8,128)S(1)} %add.14), channel_id=1, source_target_pairs={{0,8},{1,3},{2,10},{3,1},{4,12},{5,7},{6,14},{7,5},{8,0},{9,11},{1... | collective-permute-start | bytes 307208 | tf_op jit(solution)/shard_map/ppermute | solution.py:487
  85.5 1.7 %temporal_output.3 = bf16[8,2,64,1024]{3,2,1,0:T(8,128)(2,1)} custom-call(bf16[8,2,64,768]{3,2,1,0:T(8,128)(2,1)S(1)} %get-tuple-element.33.refs_0_, bf16[8,2,64,256]{3,2,1,0:T(8,128)(2,1)S(1)} %get-tuple-element.34.refs_1_, bf16[3,64,64]{2,1,0:T(8,128)(2,1)S(1)} %copy-done, ...), custom_call_target="tpu_custom_call", output_to_operand_aliasing={{}: (3, {})} | custom-call | flops 1207959552 | bytes 4194304 | tf_op jit(solution)/shard_map/temporal_output/pallas_call | solution.py:224
  87.2 1.0 %collective-permute-done.5 = f32[200,128]{1,0:T(8,128)S(1)} collective-permute-done((f32[200,128]{1,0:T(8,128)S(1)}, f32[200,128]{1,0:T(8,128)S(1)}, u32[]{:S(2)}, u32[]{:S(2)}) %collective-permute-start.5) | collective-permute-done | bytes 102432 | tf_op jit(solution)/shard_map/ppermute | solution.py:487
  88.1 0.1 collective-permute-start.6
  88.2 1.3 %collective-permute-done.6.other_ref = f32[200,128]{1,0:T(8,128)S(1)} collective-permute-done((f32[200,128]{1,0:T(8,128)S(1)}, f32[200,128]{1,0:T(8,128)S(1)}, u32[]{:S(2)}, u32[]{:S(2)}) %collective-permute-start.6) | collective-permute-done | bytes 102432 | tf_op jit(solution)/shard_map/ppermute | solution.py:560
  89.5 0.9 unpack.1
  (5 shorter events, 0.1 us)
Async XLA Ops:
  3.2 7.6 %copy-start = (bf16[3,64,64]{2,1,0:T(8,128)(2,1)S(1)}, bf16[3,64,64]{2,1,0:T(8,128)(2,1)}, u32[]{:S(2)}) copy-start(bf16[3,64,64]{2,1,0:T(8,128)(2,1)} %refs_2_.3) | copy-start | bytes 73732
  3.2 7.6 %copy-start.1 = (bf16[9,64,64]{2,1,0:T(8,128)(2,1)S(1)}, bf16[9,64,64]{2,1,0:T(8,128)(2,1)}, u32[]{:S(2)}) copy-start(bf16[9,64,64]{2,1,0:T(8,128)(2,1)} %sw_ref.1) | copy-start | bytes 221188
  3.2 7.6 %copy-start.2 = (f32[64]{0:T(128)S(1)}, f32[64]{0:T(128)}, u32[]{:S(2)}) copy-start(f32[64]{0:T(128)} %param.7) | copy-start | bytes 772
  3.2 48.6 %all-to-all-start = ((bf16[16,2,8,32,128]{4,3,2,1,0:T(8,128)(2,1)}), bf16[16,2,8,32,128]{4,3,2,1,0:T(8,128)(2,1)S(1)}, u32[]{:S(2)}, u32[]{:S(2)}) async-start(bf16[16,2,8,32,128]{4,3,2,1,0:T(8,128)(2,1)} %pack.1), calls=%async_computation | async-start | bytes 4194304 | tf_op jit(solution)/shard_map/all_to_all | solution.py:534
  51.8 1.6 %copy-start.3 = (bf16[16,64,1024]{2,1,0:T(8,128)(2,1)S(1)}, bf16[16,64,1024]{2,1,0:T(8,128)(2,1)}, u32[]{:S(2)}) copy-start(bf16[16,64,1024]{2,1,0:T(8,128)(2,1)} %get-tuple-element.25) | copy-start | bytes 6291460
  51.9 7.5 %collective-permute-start = (bf16[8,2,2,32,128]{4,3,2,1,0:T(8,128)(2,1)S(1)}, bf16[8,2,2,32,128]{4,3,2,1,0:T(8,128)(2,1)S(1)}, u32[]{:S(2)}, u32[]{:S(2)}) collective-permute-start(bf16[8,2,2,32,128]{4,3,2,1,0:T(8,128)(2,1)S(1)} %get-tuple-element.23), channel_id=1, source_target_pairs={{0,1},{1,0},{2,3},{3,2},{4,5},{5,4},{6,7},{7,6},{8,9},{9,8},{10,11... | collective-permute-start | bytes 786440 | tf_op jit(solution)/shard_map/ppermute | solution.py:541
  52.7 6.6 %collective-permute-start.1 = (bf16[8,2,2,32,128]{4,3,2,1,0:T(8,128)(2,1)S(1)}, bf16[8,2,2,32,128]{4,3,2,1,0:T(8,128)(2,1)S(1)}, u32[]{:S(2)}, u32[]{:S(2)}) collective-permute-start(bf16[8,2,2,32,128]{4,3,2,1,0:T(8,128)(2,1)S(1)} %get-tuple-element.24), channel_id=1, source_target_pairs={{2,1},{4,3},{6,5},{8,7},{10,9},{12,11},{14,13},{1,2},{3,4},{5,6},{... | collective-permute-start | bytes 786440 | tf_op jit(solution)/shard_map/ppermute | solution.py:542
  62.0 5.7 %collective-permute-start.2 = (f32[200,128]{1,0:T(8,128)S(1)}, f32[200,128]{1,0:T(8,128)S(1)}, u32[]{:S(2)}, u32[]{:S(2)}) collective-permute-start(f32[200,128]{1,0:T(8,128)S(1)} %get-tuple-element.32), channel_id=1, source_target_pairs={{0,1},{1,0},{2,3},{3,2},{4,5},{5,4},{6,7},{7,6},{8,9},{9,8},{10,11... | collective-permute-start | bytes 307208 | tf_op jit(solution)/shard_map/ppermute | solution.py:480
  67.7 7.1 %collective-permute-start.3 = (f32[200,128]{1,0:T(8,128)S(1)}, f32[200,128]{1,0:T(8,128)S(1)}, u32[]{:S(2)}, u32[]{:S(2)}) collective-permute-start(f32[200,128]{1,0:T(8,128)S(1)} %add.12), channel_id=1, source_target_pairs={{0,2},{1,5},{2,0},{3,7},{4,6},{5,1},{6,4},{7,3},{8,10},{9,13},{10,... | collective-permute-start | bytes 307208 | tf_op jit(solution)/shard_map/ppermute | solution.py:487
  74.8 7.5 %collective-permute-start.4 = (f32[200,128]{1,0:T(8,128)S(1)}, f32[200,128]{1,0:T(8,128)S(1)}, u32[]{:S(2)}, u32[]{:S(2)}) collective-permute-start(f32[200,128]{1,0:T(8,128)S(1)} %add.13), channel_id=1, source_target_pairs={{0,4},{1,9},{2,6},{3,11},{4,0},{5,13},{6,2},{7,15},{8,12},{9,1},{1... | collective-permute-start | bytes 307208 | tf_op jit(solution)/shard_map/ppermute | solution.py:487
  82.4 5.7 %collective-permute-start.5 = (f32[200,128]{1,0:T(8,128)S(1)}, f32[200,128]{1,0:T(8,128)S(1)}, u32[]{:S(2)}, u32[]{:S(2)}) collective-permute-start(f32[200,128]{1,0:T(8,128)S(1)} %add.14), channel_id=1, source_target_pairs={{0,8},{1,3},{2,10},{3,1},{4,12},{5,7},{6,14},{7,5},{8,0},{9,11},{1... | collective-permute-start | bytes 307208 | tf_op jit(solution)/shard_map/ppermute | solution.py:487
  88.1 1.4 %collective-permute-start.6 = (f32[200,128]{1,0:T(8,128)S(1)}, f32[200,128]{1,0:T(8,128)S(1)}, u32[]{:S(2)}, u32[]{:S(2)}) collective-permute-start(f32[200,128]{1,0:T(8,128)S(1)} %add.15.mine_ref), channel_id=1, source_target_pairs={{0,1},{1,0},{2,3},{3,2},{4,5},{5,4},{6,7},{7,6},{8,9},{9,8},{10,11... | collective-permute-start | bytes 307208 | tf_op jit(solution)/shard_map/ppermute | solution.py:560

commit v4 on v3

--- a/solution.py
+++ b/solution.py
@@ -273,20 +273,17 @@
             before = refs[:3]
             refs = refs[3:]
         hid_ref = refs.pop(0)
-        results = refs[: 2 if final else 3]
-        refs = refs[2 if final else 3 :]
-        gp_s, pair_s, gs_s, gb_s, cot_s, cot_sems = refs[:6]
-        refs = refs[6:]
-        cot_copies = [
-            pltpu.make_async_copy(
-                cot_ref.at[:, :, :, pl.ds(start * cols, count * cols)],
-                cot_s.at[:, :, :, pl.ds(at * cols, count * cols)],
-                cot_sems.at[p],
-            )
-            for p, (start, at, count) in enumerate(pieces_of)
-        ]
-        for copy in cot_copies:
-            copy.start()
+        results = refs[: 2 if final else 4]
+        refs = refs[2 if final else 4 :]
+        gp_s, pair_s, gs_s, gb_s = refs[:4]
+        refs = refs[4:]
+        if final:
+            cot_s = cot_ref
+        else:
+            cot_s, cot_sem = results.pop(), refs.pop(0)
+        if not final:
+            cot_copy = pltpu.make_async_copy(cot_ref, cot_s, cot_sem)
+            cot_copy.start()
 
         if halo is not None:
             top_s, bottom_s = refs[:2]
@@ -380,14 +377,23 @@
 
         lax.fori_loop(0, owners // per, some_frames, 0)
 
-        for copy in cot_copies:
-            copy.wait()
+        if not final:
+            cot_copy.wait()
+
+        def reached(f, count, j):
+            parts = [
+                cot_s[f : f + count, j, :, start * cols : (start + length) * cols]
+                for start, at, length in pieces_of
+            ]
+            joint = parts[0] if len(parts) == 1 else jnp.concatenate(parts, axis=2)
+            return joint.reshape(count * channels, pixels)
+
         pair_s[...] = jnp.zeros_like(pair_s)
         for j in range(local):
             for f in range(0, owners, near_frames):
                 count = min(ahead, owners - f)
                 pairs = lax.dot_general(
-                    cot_s[f : f + count, j].reshape(count * channels, pixels),
+                    reached(f, count, j),
                     hid_ref[f : f + near_frames, j].reshape(near_frames * channels, pixels),
                     LANES_IN_LANES,
                     preferred_element_type=F32,
@@ -432,15 +438,21 @@
                 gt_ref[k] = temporal[k]
             gb_ref[...] = gb_s[...]
 
-    view = (owners, local) + cotangent.shape[1:]
+    view = (owners, local) + cotangent.shape[-2:]
     operands = [
         lines,
-        pltpu.with_memory_space_constraint(cotangent.reshape(view), pltpu.HBM),
+        cotangent.reshape(view),
         back_grad.reshape(view),
         weights,
         bias_tile,
     ]
-    in_specs = [ON_CHIP, IN_HBM, ON_CHIP, ON_CHIP, ON_CHIP]
+    in_specs = [ON_CHIP] * len(operands)
+    if not final:
+        operands[1] = pltpu.with_memory_space_constraint(operands[1], pltpu.HBM)
+        in_specs[1] = IN_HBM
+        scratch_last = [pltpu.SemaphoreType.DMA(())]
+    else:
+        scratch_last = []
     shapes = [jax.ShapeDtypeStruct((owners, local, channels, pixels), BF16)]
     square = (trio, trio)
     slab = (taps, channels, channels)
@@ -450,9 +462,8 @@
         pltpu.VMEM((ahead * channels, near_frames * channels), F32),
         pltpu.VMEM(square, F32),
         pltpu.VMEM(tile, F32),
-        pltpu.VMEM((owners, local, channels, pixels), BF16),
-        pltpu.SemaphoreType.DMA((len(pieces_of),)),
     ]
+    scratch += scratch_last
     if halo is not None:
         operands = list(halo) + operands
         in_specs = [SCALARS, ON_CHIP, ON_CHIP] + in_specs
@@ -464,6 +475,7 @@
         scratch += [pltpu.VMEM((packed, 2 * channels), F32)]
     else:
         shapes += [jax.ShapeDtypeStruct(s, F32) for s in (square, slab, tile)]
+        shapes += [jax.ShapeDtypeStruct(view, BF16)]
     hidden, *rest = call(
         kernel,
         name,
@@ -538,13 +550,17 @@
             cotangent, temporal_weight, spatial_weight, spatial_bias.reshape(1, channels), cols
         )
         near_row, far_row = edge_rows(side, lines)
+        far = lax.ppermute(far_row, BOTH, beyond)
         near = lax.ppermute(near_row, BOTH, beside)
-        far = lax.ppermute(far_row, BOTH, beyond)
-        shared = (cotangent, back_grad, weights, bias_tile, taps)
+        shared = (back_grad, weights, bias_tile, taps)
         inside = list(range(1, rows - 1))
-        inner, *sums = layer("layer_inside", inside, lines, None, *shared, None, INSIDE_FRAMES)
+        inner, *sums, cot = layer(
+            "layer_inside", inside, lines, None, cotangent, *shared, None, INSIDE_FRAMES
+        )
         halo = (side, near, far)
-        outer, mine, other = layer("layer_edges", [0, rows - 1], lines, halo, *shared, sums, EDGE_FRAMES)
+        outer, mine, other = layer(
+            "layer_edges", [0, rows - 1], lines, halo, cot, *shared, sums, EDGE_FRAMES
+        )
         made = []
 
         def output_of(parity):

time: 90.7 us -> 90.1 us (level)
  no operation moved by 1% of the time
where the time goes in v4:
time: 90.1 us; the launch traced here: 89.8 us
  waiting for transfers between devices  43.6 us (48%)
  starting transfers between devices  25.8 us (29%)
  Pallas kernels  19.5 us (22%)
    all_to_all x1, waiting for transfers between devices, body(): lax.all_to_all(pack(frames, count), BOTH, split_axis=0, concat_axis=0, ti...  36.3 us
    ppermute x3, starting transfers between devices, sum_over_devices(): part = part + lax.ppermute(part, BOTH, pairs)  11.9 us
    pallas_call x2, Pallas kernels, layer(): call(kernel, name, tuple(shapes), 8 * (2 * 9 + taps) * channels * total *...  7.92 us
    all_to_all x1, starting transfers between devices, body(): lax.all_to_all(pack(frames, count), BOTH, split_axis=0, concat_axis=0, ti...  7.53 us
    ppermute x3, waiting for transfers between devices, sum_over_devices(): part = part + lax.ppermute(part, BOTH, pairs)  5.12 us
    pallas_call x1, Pallas kernels, prepare(): call(kernel, 'prepare', (pltpu.HBM(cotangent.shape, BF16), jax.ShapeDtype...  4.8 us
    ppermute x1, starting transfers between devices, sum_over_devices(): part = mine + lax.ppermute(other, BOTH, beside)  4.76 us
    pallas_call x2, Pallas kernels, temporal_output(): call(kernel, 'temporal_output', jax.ShapeDtypeStruct((count, 2, channels,...  3.34 us
  transfers between devices with their start and end apart: 8, of which 6 were waited for; matrix products, arithmetic and copies ran while one was open for 0% of the time, Pallas kernels for 16%

profile of v4, /device:TPU:0, one launch (start us, length us, event | category | flops | bytes accessed | tf_op | source)
XLA Modules:
  0.0 89.8 jit_solution(7693421968704511452)
XLA Ops:
  0.6 2.5 %pack.1 = bf16[16,2,8,32,128]{4,3,2,1,0:T(8,128)(2,1)} custom-call(bf16[2,32,128,128]{3,2,1,0:T(8,128)(2,1)} %images_ref.1), custom_call_target="tpu_custom_call" | custom-call | flops 1048576 | bytes 4194304 | tf_op jit(solution)/shard_map/pack/pallas_call | solution.py:75
  3.2 0.0 copy-start
  3.2 0.0 copy-start.1
  3.2 0.0 copy-start.2
  3.2 7.5 %all-to-all-start = ((bf16[16,2,8,32,128]{4,3,2,1,0:T(8,128)(2,1)}), bf16[16,2,8,32,128]{4,3,2,1,0:T(8,128)(2,1)S(1)}, u32[]{:S(2)}, u32[]{:S(2)}) async-start(bf16[16,2,8,32,128]{4,3,2,1,0:T(8,128)(2,1)} %pack.1), calls=%async_computation | async-start | bytes 4194304 | tf_op jit(solution)/shard_map/all_to_all | solution.py:546
  10.7 0.0 copy-done
  10.7 0.0 copy-done.1
  10.8 0.0 copy-done.2
  10.8 4.8 %prepare.1 = (bf16[16,64,1024]{2,1,0:T(8,128)(2,1)}, bf16[192,192]{1,0:T(8,128)(2,1)S(1)}, f32[64,128]{1,0:T(8,128)S(1)}) custom-call(bf16[16,64,1024]{2,1,0:T(8,128)(2,1)} %cot_ref.1, bf16[3,64,64]{2,1,0:T(8,128)(2,1)S(1)} %copy-done, bf16[9,64,64]{2,1,0:T(8,128)(2,1)S(1)} %copy-done.1, f32[1,64]{1,0:T(1,128)S(1)} %bitcast.10), custom_call_target="tpu_custom_call" | custom-call | flops 1610612736 | bytes 4407296 | tf_op jit(solution)/shard_map/prepare/pallas_call | solution.py:147
  15.6 36.3 %all-to-all-done = bf16[16,2,8,32,128]{4,3,2,1,0:T(8,128)(2,1)S(1)} async-done(((bf16[16,2,8,32,128]{4,3,2,1,0:T(8,128)(2,1)}), bf16[16,2,8,32,128]{4,3,2,1,0:T(8,128)(2,1)S(1)}, u32[]{:S(2)}, u32[]{:S(2)}) %all-to-all-start) | async-done | bytes 2097184 | tf_op jit(solution)/shard_map/all_to_all | solution.py:546
  51.8 0.0 copy-start.3
  51.9 0.8 collective-permute-start
  52.7 0.7 collective-permute-start.1
  53.4 0.0 copy-done.3
  53.4 5.9 %layer_inside.1 = (bf16[8,2,64,768]{3,2,1,0:T(8,128)(2,1)S(1)}, f32[192,192]{1,0:T(8,128)S(1)}, f32[3,64,64]{2,1,0:T(8,128)S(1)}, f32[64,128]{1,0:T(8,128)S(1)}, bf16[8,2,64,1024]{3,2,1,0:T(8,128)(2,1)S(1)}) custom-call(bf16[8,2,2,8,32,128]{5,4,3,2,1,0:T(8,128)(2,1)S(1)} %bitcast.8, bf16[8,2,64,1024]{3,2,1,0:T(8,128)(2,1)} %bitcast.14, ...), custom_call_target="tpu_custom_call" | custom-call | flops 8455716864 | bytes 7798784 | tf_op jit(solution)/shard_map/layer_inside/pallas_call | solution.py:479
  59.3 0.0 collective-permute-done.refs_1_
  59.4 0.0 collective-permute-done.1.refs_2_
  59.4 2.0 %layer_edges.1 = (bf16[8,2,64,256]{3,2,1,0:T(8,128)(2,1)S(1)}, f32[200,128]{1,0:T(8,128)S(1)}, f32[200,128]{1,0:T(8,128)S(1)}) custom-call(s32[1]{0:T(128)} %bitcast.side_ref.refs_0_, bf16[8,2,2,32,128]{4,3,2,1,0:T(8,128)(2,1)S(1)} %collective-permute-done.refs_1_, bf16[8,2,2,32,128]{4,3,2,1,0:T(8,128)(2,1)S(1)} %collective-permute-done.1.refs_2_, ...), custom_call_target="tpu_custom_call" | custom-call | flops 2818572288 | bytes 1458176 | tf_op jit(solution)/shard_map/layer_edges/pallas_call | solution.py:479
  61.4 4.8 %collective-permute-start.2 = (f32[200,128]{1,0:T(8,128)S(1)}, f32[200,128]{1,0:T(8,128)S(1)}, u32[]{:S(2)}, u32[]{:S(2)}) collective-permute-start(f32[200,128]{1,0:T(8,128)S(1)} %get-tuple-element.34), channel_id=1, source_target_pairs={{0,1},{1,0},{2,3},{3,2},{4,5},{5,4},{6,7},{7,6},{8,9},{9,8},{10,11... | collective-permute-start | bytes 307208 | tf_op jit(solution)/shard_map/ppermute | solution.py:492
  66.2 0.9 %collective-permute-done.2 = f32[200,128]{1,0:T(8,128)S(1)} collective-permute-done((f32[200,128]{1,0:T(8,128)S(1)}, f32[200,128]{1,0:T(8,128)S(1)}, u32[]{:S(2)}, u32[]{:S(2)}) %collective-permute-start.2) | collective-permute-done | bytes 102432 | tf_op jit(solution)/shard_map/ppermute | solution.py:492
  67.1 4.5 %collective-permute-start.3 = (f32[200,128]{1,0:T(8,128)S(1)}, f32[200,128]{1,0:T(8,128)S(1)}, u32[]{:S(2)}, u32[]{:S(2)}) collective-permute-start(f32[200,128]{1,0:T(8,128)S(1)} %add.12), channel_id=1, source_target_pairs={{0,2},{1,5},{2,0},{3,7},{4,6},{5,1},{6,4},{7,3},{8,10},{9,13},{10,... | collective-permute-start | bytes 307208 | tf_op jit(solution)/shard_map/ppermute | solution.py:499
  71.6 2.6 %collective-permute-done.3 = f32[200,128]{1,0:T(8,128)S(1)} collective-permute-done((f32[200,128]{1,0:T(8,128)S(1)}, f32[200,128]{1,0:T(8,128)S(1)}, u32[]{:S(2)}, u32[]{:S(2)}) %collective-permute-start.3) | collective-permute-done | bytes 102432 | tf_op jit(solution)/shard_map/ppermute | solution.py:499
  74.2 4.4 %collective-permute-start.4 = (f32[200,128]{1,0:T(8,128)S(1)}, f32[200,128]{1,0:T(8,128)S(1)}, u32[]{:S(2)}, u32[]{:S(2)}) collective-permute-start(f32[200,128]{1,0:T(8,128)S(1)} %add.13), channel_id=1, source_target_pairs={{0,4},{1,9},{2,6},{3,11},{4,0},{5,13},{6,2},{7,15},{8,12},{9,1},{1... | collective-permute-start | bytes 307208 | tf_op jit(solution)/shard_map/ppermute | solution.py:499
  78.6 1.7 %temporal_output.2.refs_3_ = bf16[8,2,64,1024]{3,2,1,0:T(8,128)(2,1)} custom-call(bf16[8,2,64,768]{3,2,1,0:T(8,128)(2,1)S(1)} %get-tuple-element.35.refs_0_, bf16[8,2,64,256]{3,2,1,0:T(8,128)(2,1)S(1)} %get-tuple-element.36.refs_1_, bf16[3,64,64]{2,1,0:T(8,128)(2,1)S(1)} %copy-done), custom_call_target="tpu_custom_call" | custom-call | flops 1207959552 | bytes 4194304 | tf_op jit(solution)/shard_map/temporal_output/pallas_call | solution.py:224
  80.3 1.5 %collective-permute-done.4 = f32[200,128]{1,0:T(8,128)S(1)} collective-permute-done((f32[200,128]{1,0:T(8,128)S(1)}, f32[200,128]{1,0:T(8,128)S(1)}, u32[]{:S(2)}, u32[]{:S(2)}) %collective-permute-start.4) | collective-permute-done | bytes 102432 | tf_op jit(solution)/shard_map/ppermute | solution.py:499
  81.8 3.1 %collective-permute-start.5 = (f32[200,128]{1,0:T(8,128)S(1)}, f32[200,128]{1,0:T(8,128)S(1)}, u32[]{:S(2)}, u32[]{:S(2)}) collective-permute-start(f32[200,128]{1,0:T(8,128)S(1)} %add.14), channel_id=1, source_target_pairs={{0,8},{1,3},{2,10},{3,1},{4,12},{5,7},{6,14},{7,5},{8,0},{9,11},{1... | collective-permute-start | bytes 307208 | tf_op jit(solution)/shard_map/ppermute | solution.py:499
  84.9 1.7 %temporal_output.3 = bf16[8,2,64,1024]{3,2,1,0:T(8,128)(2,1)} custom-call(bf16[8,2,64,768]{3,2,1,0:T(8,128)(2,1)S(1)} %get-tuple-element.35.refs_0_, bf16[8,2,64,256]{3,2,1,0:T(8,128)(2,1)S(1)} %get-tuple-element.36.refs_1_, bf16[3,64,64]{2,1,0:T(8,128)(2,1)S(1)} %copy-done, ...), custom_call_target="tpu_custom_call", output_to_operand_aliasing={{}: (3, {})} | custom-call | flops 1207959552 | bytes 4194304 | tf_op jit(solution)/shard_map/temporal_output/pallas_call | solution.py:224
  86.6 1.0 %collective-permute-done.5 = f32[200,128]{1,0:T(8,128)S(1)} collective-permute-done((f32[200,128]{1,0:T(8,128)S(1)}, f32[200,128]{1,0:T(8,128)S(1)}, u32[]{:S(2)}, u32[]{:S(2)}) %collective-permute-start.5) | collective-permute-done | bytes 102432 | tf_op jit(solution)/shard_map/ppermute | solution.py:499
  87.6 0.1 collective-permute-start.6
  87.7 1.3 %collective-permute-done.6.other_ref = f32[200,128]{1,0:T(8,128)S(1)} collective-permute-done((f32[200,128]{1,0:T(8,128)S(1)}, f32[200,128]{1,0:T(8,128)S(1)}, u32[]{:S(2)}, u32[]{:S(2)}) %collective-permute-start.6) | collective-permute-done | bytes 102432 | tf_op jit(solution)/shard_map/ppermute | solution.py:576
  88.9 0.9 unpack.1
  (5 shorter events, 0.1 us)
Async XLA Ops:
  3.2 7.6 %copy-start = (bf16[3,64,64]{2,1,0:T(8,128)(2,1)S(1)}, bf16[3,64,64]{2,1,0:T(8,128)(2,1)}, u32[]{:S(2)}) copy-start(bf16[3,64,64]{2,1,0:T(8,128)(2,1)} %refs_2_.3) | copy-start | bytes 73732
  3.2 7.6 %copy-start.1 = (bf16[9,64,64]{2,1,0:T(8,128)(2,1)S(1)}, bf16[9,64,64]{2,1,0:T(8,128)(2,1)}, u32[]{:S(2)}) copy-start(bf16[9,64,64]{2,1,0:T(8,128)(2,1)} %sw_ref.1) | copy-start | bytes 221188
  3.2 7.6 %copy-start.2 = (f32[64]{0:T(128)S(1)}, f32[64]{0:T(128)}, u32[]{:S(2)}) copy-start(f32[64]{0:T(128)} %param.7) | copy-start | bytes 772
  3.2 48.6 %all-to-all-start = ((bf16[16,2,8,32,128]{4,3,2,1,0:T(8,128)(2,1)}), bf16[16,2,8,32,128]{4,3,2,1,0:T(8,128)(2,1)S(1)}, u32[]{:S(2)}, u32[]{:S(2)}) async-start(bf16[16,2,8,32,128]{4,3,2,1,0:T(8,128)(2,1)} %pack.1), calls=%async_computation | async-start | bytes 4194304 | tf_op jit(solution)/shard_map/all_to_all | solution.py:546
  51.8 1.6 %copy-start.3 = (bf16[16,64,1024]{2,1,0:T(8,128)(2,1)S(1)}, bf16[16,64,1024]{2,1,0:T(8,128)(2,1)}, u32[]{:S(2)}) copy-start(bf16[16,64,1024]{2,1,0:T(8,128)(2,1)} %get-tuple-element.26) | copy-start | bytes 6291460
  51.9 7.5 %collective-permute-start = (bf16[8,2,2,32,128]{4,3,2,1,0:T(8,128)(2,1)S(1)}, bf16[8,2,2,32,128]{4,3,2,1,0:T(8,128)(2,1)S(1)}, u32[]{:S(2)}, u32[]{:S(2)}) collective-permute-start(bf16[8,2,2,32,128]{4,3,2,1,0:T(8,128)(2,1)S(1)} %get-tuple-element.24), channel_id=1, source_target_pairs={{0,1},{1,0},{2,3},{3,2},{4,5},{5,4},{6,7},{7,6},{8,9},{9,8},{10,11... | collective-permute-start | bytes 786440 | tf_op jit(solution)/shard_map/ppermute | solution.py:554
  52.7 6.6 %collective-permute-start.1 = (bf16[8,2,2,32,128]{4,3,2,1,0:T(8,128)(2,1)S(1)}, bf16[8,2,2,32,128]{4,3,2,1,0:T(8,128)(2,1)S(1)}, u32[]{:S(2)}, u32[]{:S(2)}) collective-permute-start(bf16[8,2,2,32,128]{4,3,2,1,0:T(8,128)(2,1)S(1)} %get-tuple-element.25), channel_id=1, source_target_pairs={{2,1},{4,3},{6,5},{8,7},{10,9},{12,11},{14,13},{1,2},{3,4},{5,6},{... | collective-permute-start | bytes 786440 | tf_op jit(solution)/shard_map/ppermute | solution.py:553
  61.4 5.7 %collective-permute-start.2 = (f32[200,128]{1,0:T(8,128)S(1)}, f32[200,128]{1,0:T(8,128)S(1)}, u32[]{:S(2)}, u32[]{:S(2)}) collective-permute-start(f32[200,128]{1,0:T(8,128)S(1)} %get-tuple-element.34), channel_id=1, source_target_pairs={{0,1},{1,0},{2,3},{3,2},{4,5},{5,4},{6,7},{7,6},{8,9},{9,8},{10,11... | collective-permute-start | bytes 307208 | tf_op jit(solution)/shard_map/ppermute | solution.py:492
  67.1 7.1 %collective-permute-start.3 = (f32[200,128]{1,0:T(8,128)S(1)}, f32[200,128]{1,0:T(8,128)S(1)}, u32[]{:S(2)}, u32[]{:S(2)}) collective-permute-start(f32[200,128]{1,0:T(8,128)S(1)} %add.12), channel_id=1, source_target_pairs={{0,2},{1,5},{2,0},{3,7},{4,6},{5,1},{6,4},{7,3},{8,10},{9,13},{10,... | collective-permute-start | bytes 307208 | tf_op jit(solution)/shard_map/ppermute | solution.py:499
  74.2 7.5 %collective-permute-start.4 = (f32[200,128]{1,0:T(8,128)S(1)}, f32[200,128]{1,0:T(8,128)S(1)}, u32[]{:S(2)}, u32[]{:S(2)}) collective-permute-start(f32[200,128]{1,0:T(8,128)S(1)} %add.13), channel_id=1, source_target_pairs={{0,4},{1,9},{2,6},{3,11},{4,0},{5,13},{6,2},{7,15},{8,12},{9,1},{1... | collective-permute-start | bytes 307208 | tf_op jit(solution)/shard_map/ppermute | solution.py:499
  81.8 5.8 %collective-permute-start.5 = (f32[200,128]{1,0:T(8,128)S(1)}, f32[200,128]{1,0:T(8,128)S(1)}, u32[]{:S(2)}, u32[]{:S(2)}) collective-permute-start(f32[200,128]{1,0:T(8,128)S(1)} %add.14), channel_id=1, source_target_pairs={{0,8},{1,3},{2,10},{3,1},{4,12},{5,7},{6,14},{7,5},{8,0},{9,11},{1... | collective-permute-start | bytes 307208 | tf_op jit(solution)/shard_map/ppermute | solution.py:499
  87.6 1.4 %collective-permute-start.6 = (f32[200,128]{1,0:T(8,128)S(1)}, f32[200,128]{1,0:T(8,128)S(1)}, u32[]{:S(2)}, u32[]{:S(2)}) collective-permute-start(f32[200,128]{1,0:T(8,128)S(1)} %add.15.mine_ref), channel_id=1, source_target_pairs={{0,1},{1,0},{2,3},{3,2},{4,5},{5,4},{6,7},{7,6},{8,9},{9,8},{10,11... | collective-permute-start | bytes 307208 | tf_op jit(solution)/shard_map/ppermute | solution.py:576

commit v5 on v4

--- a/solution.py
+++ b/solution.py
@@ -497,7 +497,7 @@
             (2 * f + c, 2 * (f ^ orders[c][stage]) + c) for f in range(owners) for c in range(2)
         ]
         part = part + lax.ppermute(part, BOTH, pairs)
-        if stage > 0 and beneath:
+        if beneath:
             part = beneath.pop(0)(part)
     return part
 

time: 90.1 us -> 90.1 us (level)
  no operation moved by 1% of the time
where the time goes in v5:
time: 90.1 us; the launch traced here: 89.8 us
  waiting for transfers between devices  43.6 us (48%)
  starting transfers between devices  25.8 us (29%)
  Pallas kernels  19.5 us (22%)
    all_to_all x1, waiting for transfers between devices, body(): lax.all_to_all(pack(frames, count), BOTH, split_axis=0, concat_axis=0, ti...  36.3 us
    ppermute x3, starting transfers between devices, sum_over_devices(): part = part + lax.ppermute(part, BOTH, pairs)  11.9 us
    pallas_call x2, Pallas kernels, layer(): call(kernel, name, tuple(shapes), 8 * (2 * 9 + taps) * channels * total *...  7.91 us
    all_to_all x1, starting transfers between devices, body(): lax.all_to_all(pack(frames, count), BOTH, split_axis=0, concat_axis=0, ti...  7.53 us
    ppermute x3, waiting for transfers between devices, sum_over_devices(): part = part + lax.ppermute(part, BOTH, pairs)  5.11 us
    pallas_call x1, Pallas kernels, prepare(): call(kernel, 'prepare', (pltpu.HBM(cotangent.shape, BF16), jax.ShapeDtype...  4.8 us
    ppermute x1, starting transfers between devices, sum_over_devices(): part = mine + lax.ppermute(other, BOTH, beside)  4.76 us
    pallas_call x2, Pallas kernels, temporal_output(): call(kernel, 'temporal_output', jax.ShapeDtypeStruct((count, 2, channels,...  3.35 us
  transfers between devices with their start and end apart: 8, of which 6 were waited for; matrix products, arithmetic and copies ran while one was open for 0% of the time, Pallas kernels for 16%

profile of v5, /device:TPU:0, one launch (start us, length us, event | category | flops | bytes accessed | tf_op | source)
XLA Modules:
  0.0 89.8 jit_solution(8689848655800669643)
XLA Ops:
  0.6 2.5 %pack.1 = bf16[16,2,8,32,128]{4,3,2,1,0:T(8,128)(2,1)} custom-call(bf16[2,32,128,128]{3,2,1,0:T(8,128)(2,1)} %images_ref.1), custom_call_target="tpu_custom_call" | custom-call | flops 1048576 | bytes 4194304 | tf_op jit(solution)/shard_map/pack/pallas_call | solution.py:75
  3.2 0.0 copy-start
  3.2 0.0 copy-start.1
  3.2 0.0 copy-start.2
  3.2 7.5 %all-to-all-start = ((bf16[16,2,8,32,128]{4,3,2,1,0:T(8,128)(2,1)}), bf16[16,2,8,32,128]{4,3,2,1,0:T(8,128)(2,1)S(1)}, u32[]{:S(2)}, u32[]{:S(2)}) async-start(bf16[16,2,8,32,128]{4,3,2,1,0:T(8,128)(2,1)} %pack.1), calls=%async_computation | async-start | bytes 4194304 | tf_op jit(solution)/shard_map/all_to_all | solution.py:546
  10.7 0.0 copy-done
  10.7 0.0 copy-done.1
  10.8 0.0 copy-done.2
  10.8 4.8 %prepare.1 = (bf16[16,64,1024]{2,1,0:T(8,128)(2,1)}, bf16[192,192]{1,0:T(8,128)(2,1)S(1)}, f32[64,128]{1,0:T(8,128)S(1)}) custom-call(bf16[16,64,1024]{2,1,0:T(8,128)(2,1)} %cot_ref.1, bf16[3,64,64]{2,1,0:T(8,128)(2,1)S(1)} %copy-done, bf16[9,64,64]{2,1,0:T(8,128)(2,1)S(1)} %copy-done.1, f32[1,64]{1,0:T(1,128)S(1)} %bitcast.10), custom_call_target="tpu_custom_call" | custom-call | flops 1610612736 | bytes 4407296 | tf_op jit(solution)/shard_map/prepare/pallas_call | solution.py:147
  15.6 36.3 %all-to-all-done = bf16[16,2,8,32,128]{4,3,2,1,0:T(8,128)(2,1)S(1)} async-done(((bf16[16,2,8,32,128]{4,3,2,1,0:T(8,128)(2,1)}), bf16[16,2,8,32,128]{4,3,2,1,0:T(8,128)(2,1)S(1)}, u32[]{:S(2)}, u32[]{:S(2)}) %all-to-all-start) | async-done | bytes 2097184 | tf_op jit(solution)/shard_map/all_to_all | solution.py:546
  51.8 0.0 copy-start.3
  51.9 0.8 collective-permute-start
  52.7 0.7 collective-permute-start.1
  53.4 0.0 copy-done.3
  53.4 5.9 %layer_inside.1 = (bf16[8,2,64,768]{3,2,1,0:T(8,128)(2,1)S(1)}, f32[192,192]{1,0:T(8,128)S(1)}, f32[3,64,64]{2,1,0:T(8,128)S(1)}, f32[64,128]{1,0:T(8,128)S(1)}, bf16[8,2,64,1024]{3,2,1,0:T(8,128)(2,1)S(1)}) custom-call(bf16[8,2,2,8,32,128]{5,4,3,2,1,0:T(8,128)(2,1)S(1)} %bitcast.8, bf16[8,2,64,1024]{3,2,1,0:T(8,128)(2,1)} %bitcast.14, ...), custom_call_target="tpu_custom_call" | custom-call | flops 8455716864 | bytes 7798784 | tf_op jit(solution)/shard_map/layer_inside/pallas_call | solution.py:479
  59.3 0.0 collective-permute-done.refs_1_
  59.4 0.0 collective-permute-done.1.refs_2_
  59.4 2.0 %layer_edges.1 = (bf16[8,2,64,256]{3,2,1,0:T(8,128)(2,1)S(1)}, f32[200,128]{1,0:T(8,128)S(1)}, f32[200,128]{1,0:T(8,128)S(1)}) custom-call(s32[1]{0:T(128)} %bitcast.side_ref.refs_0_, bf16[8,2,2,32,128]{4,3,2,1,0:T(8,128)(2,1)S(1)} %collective-permute-done.refs_1_, bf16[8,2,2,32,128]{4,3,2,1,0:T(8,128)(2,1)S(1)} %collective-permute-done.1.refs_2_, ...), custom_call_target="tpu_custom_call" | custom-call | flops 2818572288 | bytes 1458176 | tf_op jit(solution)/shard_map/layer_edges/pallas_call | solution.py:479
  61.4 4.8 %collective-permute-start.2 = (f32[200,128]{1,0:T(8,128)S(1)}, f32[200,128]{1,0:T(8,128)S(1)}, u32[]{:S(2)}, u32[]{:S(2)}) collective-permute-start(f32[200,128]{1,0:T(8,128)S(1)} %get-tuple-element.34), channel_id=1, source_target_pairs={{0,1},{1,0},{2,3},{3,2},{4,5},{5,4},{6,7},{7,6},{8,9},{9,8},{10,11... | collective-permute-start | bytes 307208 | tf_op jit(solution)/shard_map/ppermute | solution.py:492
  66.1 0.9 %collective-permute-done.2 = f32[200,128]{1,0:T(8,128)S(1)} collective-permute-done((f32[200,128]{1,0:T(8,128)S(1)}, f32[200,128]{1,0:T(8,128)S(1)}, u32[]{:S(2)}, u32[]{:S(2)}) %collective-permute-start.2) | collective-permute-done | bytes 102432 | tf_op jit(solution)/shard_map/ppermute | solution.py:492
  67.1 4.5 %collective-permute-start.3 = (f32[200,128]{1,0:T(8,128)S(1)}, f32[200,128]{1,0:T(8,128)S(1)}, u32[]{:S(2)}, u32[]{:S(2)}) collective-permute-start(f32[200,128]{1,0:T(8,128)S(1)} %add.12), channel_id=1, source_target_pairs={{0,2},{1,5},{2,0},{3,7},{4,6},{5,1},{6,4},{7,3},{8,10},{9,13},{10,... | collective-permute-start | bytes 307208 | tf_op jit(solution)/shard_map/ppermute | solution.py:499
  71.6 1.7 %temporal_output.2.refs_3_ = bf16[8,2,64,1024]{3,2,1,0:T(8,128)(2,1)} custom-call(bf16[8,2,64,768]{3,2,1,0:T(8,128)(2,1)S(1)} %get-tuple-element.35.refs_0_, bf16[8,2,64,256]{3,2,1,0:T(8,128)(2,1)S(1)} %get-tuple-element.36.refs_1_, bf16[3,64,64]{2,1,0:T(8,128)(2,1)S(1)} %copy-done), custom_call_target="tpu_custom_call" | custom-call | flops 1207959552 | bytes 4194304 | tf_op jit(solution)/shard_map/temporal_output/pallas_call | solution.py:224
  73.3 1.0 %collective-permute-done.3 = f32[200,128]{1,0:T(8,128)S(1)} collective-permute-done((f32[200,128]{1,0:T(8,128)S(1)}, f32[200,128]{1,0:T(8,128)S(1)}, u32[]{:S(2)}, u32[]{:S(2)}) %collective-permute-start.3) | collective-permute-done | bytes 102432 | tf_op jit(solution)/shard_map/ppermute | solution.py:499
  74.2 4.4 %collective-permute-start.4 = (f32[200,128]{1,0:T(8,128)S(1)}, f32[200,128]{1,0:T(8,128)S(1)}, u32[]{:S(2)}, u32[]{:S(2)}) collective-permute-start(f32[200,128]{1,0:T(8,128)S(1)} %add.13), channel_id=1, source_target_pairs={{0,4},{1,9},{2,6},{3,11},{4,0},{5,13},{6,2},{7,15},{8,12},{9,1},{1... | collective-permute-start | bytes 307208 | tf_op jit(solution)/shard_map/ppermute | solution.py:499
  78.6 1.7 %temporal_output.3 = bf16[8,2,64,1024]{3,2,1,0:T(8,128)(2,1)} custom-call(bf16[8,2,64,768]{3,2,1,0:T(8,128)(2,1)S(1)} %get-tuple-element.35.refs_0_, bf16[8,2,64,256]{3,2,1,0:T(8,128)(2,1)S(1)} %get-tuple-element.36.refs_1_, bf16[3,64,64]{2,1,0:T(8,128)(2,1)S(1)} %copy-done, ...), custom_call_target="tpu_custom_call", output_to_operand_aliasing={{}: (3, {})} | custom-call | flops 1207959552 | bytes 4194304 | tf_op jit(solution)/shard_map/temporal_output/pallas_call | solution.py:224
  80.3 1.5 %collective-permute-done.4 = f32[200,128]{1,0:T(8,128)S(1)} collective-permute-done((f32[200,128]{1,0:T(8,128)S(1)}, f32[200,128]{1,0:T(8,128)S(1)}, u32[]{:S(2)}, u32[]{:S(2)}) %collective-permute-start.4) | collective-permute-done | bytes 102432 | tf_op jit(solution)/shard_map/ppermute | solution.py:499
  81.8 3.1 %collective-permute-start.5 = (f32[200,128]{1,0:T(8,128)S(1)}, f32[200,128]{1,0:T(8,128)S(1)}, u32[]{:S(2)}, u32[]{:S(2)}) collective-permute-start(f32[200,128]{1,0:T(8,128)S(1)} %add.14), channel_id=1, source_target_pairs={{0,8},{1,3},{2,10},{3,1},{4,12},{5,7},{6,14},{7,5},{8,0},{9,11},{1... | collective-permute-start | bytes 307208 | tf_op jit(solution)/shard_map/ppermute | solution.py:499
  84.9 2.6 %collective-permute-done.5 = f32[200,128]{1,0:T(8,128)S(1)} collective-permute-done((f32[200,128]{1,0:T(8,128)S(1)}, f32[200,128]{1,0:T(8,128)S(1)}, u32[]{:S(2)}, u32[]{:S(2)}) %collective-permute-start.5) | collective-permute-done | bytes 102432 | tf_op jit(solution)/shard_map/ppermute | solution.py:499
  87.6 0.1 collective-permute-start.6
  87.6 1.3 %collective-permute-done.6.other_ref = f32[200,128]{1,0:T(8,128)S(1)} collective-permute-done((f32[200,128]{1,0:T(8,128)S(1)}, f32[200,128]{1,0:T(8,128)S(1)}, u32[]{:S(2)}, u32[]{:S(2)}) %collective-permute-start.6) | collective-permute-done | bytes 102432 | tf_op jit(solution)/shard_map/ppermute | solution.py:576
  88.9 0.9 unpack.1
  (5 shorter events, 0.1 us)
Async XLA Ops:
  3.2 7.6 %copy-start = (bf16[3,64,64]{2,1,0:T(8,128)(2,1)S(1)}, bf16[3,64,64]{2,1,0:T(8,128)(2,1)}, u32[]{:S(2)}) copy-start(bf16[3,64,64]{2,1,0:T(8,128)(2,1)} %refs_2_.3) | copy-start | bytes 73732
  3.2 7.6 %copy-start.1 = (bf16[9,64,64]{2,1,0:T(8,128)(2,1)S(1)}, bf16[9,64,64]{2,1,0:T(8,128)(2,1)}, u32[]{:S(2)}) copy-start(bf16[9,64,64]{2,1,0:T(8,128)(2,1)} %sw_ref.1) | copy-start | bytes 221188
  3.2 7.6 %copy-start.2 = (f32[64]{0:T(128)S(1)}, f32[64]{0:T(128)}, u32[]{:S(2)}) copy-start(f32[64]{0:T(128)} %param.7) | copy-start | bytes 772
  3.2 48.6 %all-to-all-start = ((bf16[16,2,8,32,128]{4,3,2,1,0:T(8,128)(2,1)}), bf16[16,2,8,32,128]{4,3,2,1,0:T(8,128)(2,1)S(1)}, u32[]{:S(2)}, u32[]{:S(2)}) async-start(bf16[16,2,8,32,128]{4,3,2,1,0:T(8,128)(2,1)} %pack.1), calls=%async_computation | async-start | bytes 4194304 | tf_op jit(solution)/shard_map/all_to_all | solution.py:546
  51.8 1.6 %copy-start.3 = (bf16[16,64,1024]{2,1,0:T(8,128)(2,1)S(1)}, bf16[16,64,1024]{2,1,0:T(8,128)(2,1)}, u32[]{:S(2)}) copy-start(bf16[16,64,1024]{2,1,0:T(8,128)(2,1)} %get-tuple-element.26) | copy-start | bytes 6291460
  51.9 7.5 %collective-permute-start = (bf16[8,2,2,32,128]{4,3,2,1,0:T(8,128)(2,1)S(1)}, bf16[8,2,2,32,128]{4,3,2,1,0:T(8,128)(2,1)S(1)}, u32[]{:S(2)}, u32[]{:S(2)}) collective-permute-start(bf16[8,2,2,32,128]{4,3,2,1,0:T(8,128)(2,1)S(1)} %get-tuple-element.24), channel_id=1, source_target_pairs={{0,1},{1,0},{2,3},{3,2},{4,5},{5,4},{6,7},{7,6},{8,9},{9,8},{10,11... | collective-permute-start | bytes 786440 | tf_op jit(solution)/shard_map/ppermute | solution.py:554
  52.7 6.6 %collective-permute-start.1 = (bf16[8,2,2,32,128]{4,3,2,1,0:T(8,128)(2,1)S(1)}, bf16[8,2,2,32,128]{4,3,2,1,0:T(8,128)(2,1)S(1)}, u32[]{:S(2)}, u32[]{:S(2)}) collective-permute-start(bf16[8,2,2,32,128]{4,3,2,1,0:T(8,128)(2,1)S(1)} %get-tuple-element.25), channel_id=1, source_target_pairs={{2,1},{4,3},{6,5},{8,7},{10,9},{12,11},{14,13},{1,2},{3,4},{5,6},{... | collective-permute-start | bytes 786440 | tf_op jit(solution)/shard_map/ppermute | solution.py:553
  61.4 5.7 %collective-permute-start.2 = (f32[200,128]{1,0:T(8,128)S(1)}, f32[200,128]{1,0:T(8,128)S(1)}, u32[]{:S(2)}, u32[]{:S(2)}) collective-permute-start(f32[200,128]{1,0:T(8,128)S(1)} %get-tuple-element.34), channel_id=1, source_target_pairs={{0,1},{1,0},{2,3},{3,2},{4,5},{5,4},{6,7},{7,6},{8,9},{9,8},{10,11... | collective-permute-start | bytes 307208 | tf_op jit(solution)/shard_map/ppermute | solution.py:492
  67.1 7.1 %collective-permute-start.3 = (f32[200,128]{1,0:T(8,128)S(1)}, f32[200,128]{1,0:T(8,128)S(1)}, u32[]{:S(2)}, u32[]{:S(2)}) collective-permute-start(f32[200,128]{1,0:T(8,128)S(1)} %add.12), channel_id=1, source_target_pairs={{0,2},{1,5},{2,0},{3,7},{4,6},{5,1},{6,4},{7,3},{8,10},{9,13},{10,... | collective-permute-start | bytes 307208 | tf_op jit(solution)/shard_map/ppermute | solution.py:499
  74.2 7.5 %collective-permute-start.4 = (f32[200,128]{1,0:T(8,128)S(1)}, f32[200,128]{1,0:T(8,128)S(1)}, u32[]{:S(2)}, u32[]{:S(2)}) collective-permute-start(f32[200,128]{1,0:T(8,128)S(1)} %add.13), channel_id=1, source_target_pairs={{0,4},{1,9},{2,6},{3,11},{4,0},{5,13},{6,2},{7,15},{8,12},{9,1},{1... | collective-permute-start | bytes 307208 | tf_op jit(solution)/shard_map/ppermute | solution.py:499
  81.8 5.7 %collective-permute-start.5 = (f32[200,128]{1,0:T(8,128)S(1)}, f32[200,128]{1,0:T(8,128)S(1)}, u32[]{:S(2)}, u32[]{:S(2)}) collective-permute-start(f32[200,128]{1,0:T(8,128)S(1)} %add.14), channel_id=1, source_target_pairs={{0,8},{1,3},{2,10},{3,1},{4,12},{5,7},{6,14},{7,5},{8,0},{9,11},{1... | collective-permute-start | bytes 307208 | tf_op jit(solution)/shard_map/ppermute | solution.py:499
  87.6 1.4 %collective-permute-start.6 = (f32[200,128]{1,0:T(8,128)S(1)}, f32[200,128]{1,0:T(8,128)S(1)}, u32[]{:S(2)}, u32[]{:S(2)}) collective-permute-start(f32[200,128]{1,0:T(8,128)S(1)} %add.15.mine_ref), channel_id=1, source_target_pairs={{0,1},{1,0},{2,3},{3,2},{4,5},{5,4},{6,7},{7,6},{8,9},{9,8},{10,11... | collective-permute-start | bytes 307208 | tf_op jit(solution)/shard_map/ppermute | solution.py:576

commit v6 on v4

--- a/solution.py
+++ b/solution.py
@@ -388,17 +388,25 @@
             joint = parts[0] if len(parts) == 1 else jnp.concatenate(parts, axis=2)
             return joint.reshape(count * channels, pixels)
 
-        pair_s[...] = jnp.zeros_like(pair_s)
-        for j in range(local):
-            for f in range(0, owners, near_frames):
-                count = min(ahead, owners - f)
-                pairs = lax.dot_general(
-                    reached(f, count, j),
-                    hid_ref[f : f + near_frames, j].reshape(near_frames * channels, pixels),
-                    LANES_IN_LANES,
-                    preferred_element_type=F32,
-                )
+        for f in range(0, owners, near_frames):
+            count = min(ahead, owners - f)
+            reach = jnp.concatenate([reached(f, count, j) for j in range(local)], axis=1)
+            delayed = jnp.concatenate(
+                [
+                    hid_ref[f : f + near_frames, j].reshape(near_frames * channels, pixels)
+                    for j in range(local)
+                ],
+                axis=1,
+            )
+            pairs = lax.dot_general(
+                reach, delayed, LANES_IN_LANES, preferred_element_type=F32
+            )
+            if f > 0:
                 pair_s[0 : count * channels] += pairs
+            else:
+                pair_s[0 : count * channels] = pairs
+                if count < ahead:
+                    pair_s[count * channels :] = jnp.zeros_like(pair_s[count * channels :])
         temporal = []
         for k in range(taps):
             block = None

time: 90.1 us -> 90.1 us (level)
  no operation moved by 1% of the time
where the time goes in v6:
time: 90.1 us; the launch traced here: 89.8 us
  waiting for transfers between devices  43.6 us (48%)
  starting transfers between devices  25.8 us (29%)
  Pallas kernels  19.5 us (22%)
    all_to_all x1, waiting for transfers between devices, body(): lax.all_to_all(pack(frames, count), BOTH, split_axis=0, concat_axis=0, ti...  36.3 us
    ppermute x3, starting transfers between devices, sum_over_devices(): part = part + lax.ppermute(part, BOTH, pairs)  11.9 us
    pallas_call x2, Pallas kernels, layer(): call(kernel, name, tuple(shapes), 8 * (2 * 9 + taps) * channels * total *...  7.9 us
    all_to_all x1, starting transfers between devices, body(): lax.all_to_all(pack(frames, count), BOTH, split_axis=0, concat_axis=0, ti...  7.53 us
    ppermute x3, waiting for transfers between devices, sum_over_devices(): part = part + lax.ppermute(part, BOTH, pairs)  5.09 us
    pallas_call x1, Pallas kernels, prepare(): call(kernel, 'prepare', (pltpu.HBM(cotangent.shape, BF16), jax.ShapeDtype...  4.8 us
    ppermute x1, starting transfers between devices, sum_over_devices(): part = mine + lax.ppermute(other, BOTH, beside)  4.76 us
    pallas_call x2, Pallas kernels, temporal_output(): call(kernel, 'temporal_output', jax.ShapeDtypeStruct((count, 2, channels,...  3.37 us
  transfers between devices with their start and end apart: 8, of which 6 were waited for; matrix products, arithmetic and copies ran while one was open for 0% of the time, Pallas kernels for 16%

profile of v6, /device:TPU:0, one launch (start us, length us, event | category | flops | bytes accessed | tf_op | source)
XLA Modules:
  0.0 89.8 jit_solution(16647866488883041195)
XLA Ops:
  0.6 2.5 %pack.1 = bf16[16,2,8,32,128]{4,3,2,1,0:T(8,128)(2,1)} custom-call(bf16[2,32,128,128]{3,2,1,0:T(8,128)(2,1)} %images_ref.1), custom_call_target="tpu_custom_call" | custom-call | flops 1048576 | bytes 4194304 | tf_op jit(solution)/shard_map/pack/pallas_call | solution.py:75
  3.2 0.0 copy-start
  3.2 0.0 copy-start.1
  3.2 0.0 copy-start.2
  3.2 7.5 %all-to-all-start = ((bf16[16,2,8,32,128]{4,3,2,1,0:T(8,128)(2,1)}), bf16[16,2,8,32,128]{4,3,2,1,0:T(8,128)(2,1)S(1)}, u32[]{:S(2)}, u32[]{:S(2)}) async-start(bf16[16,2,8,32,128]{4,3,2,1,0:T(8,128)(2,1)} %pack.1), calls=%async_computation | async-start | bytes 4194304 | tf_op jit(solution)/shard_map/all_to_all | solution.py:554
  10.7 0.0 copy-done
  10.7 0.0 copy-done.1
  10.8 0.0 copy-done.2
  10.8 4.8 %prepare.1 = (bf16[16,64,1024]{2,1,0:T(8,128)(2,1)}, bf16[192,192]{1,0:T(8,128)(2,1)S(1)}, f32[64,128]{1,0:T(8,128)S(1)}) custom-call(bf16[16,64,1024]{2,1,0:T(8,128)(2,1)} %cot_ref.1, bf16[3,64,64]{2,1,0:T(8,128)(2,1)S(1)} %copy-done, bf16[9,64,64]{2,1,0:T(8,128)(2,1)S(1)} %copy-done.1, f32[1,64]{1,0:T(1,128)S(1)} %bitcast.10), custom_call_target="tpu_custom_call" | custom-call | flops 1610612736 | bytes 4407296 | tf_op jit(solution)/shard_map/prepare/pallas_call | solution.py:147
  15.6 36.3 %all-to-all-done = bf16[16,2,8,32,128]{4,3,2,1,0:T(8,128)(2,1)S(1)} async-done(((bf16[16,2,8,32,128]{4,3,2,1,0:T(8,128)(2,1)}), bf16[16,2,8,32,128]{4,3,2,1,0:T(8,128)(2,1)S(1)}, u32[]{:S(2)}, u32[]{:S(2)}) %all-to-all-start) | async-done | bytes 2097184 | tf_op jit(solution)/shard_map/all_to_all | solution.py:554
  51.8 0.0 copy-start.3
  51.9 0.8 collective-permute-start
  52.7 0.7 collective-permute-start.1
  53.4 0.0 copy-done.3
  53.4 5.9 %layer_inside.1 = (bf16[8,2,64,768]{3,2,1,0:T(8,128)(2,1)S(1)}, f32[192,192]{1,0:T(8,128)S(1)}, f32[3,64,64]{2,1,0:T(8,128)S(1)}, f32[64,128]{1,0:T(8,128)S(1)}, bf16[8,2,64,1024]{3,2,1,0:T(8,128)(2,1)S(1)}) custom-call(bf16[8,2,2,8,32,128]{5,4,3,2,1,0:T(8,128)(2,1)S(1)} %bitcast.8, bf16[8,2,64,1024]{3,2,1,0:T(8,128)(2,1)} %bitcast.14, ...), custom_call_target="tpu_custom_call" | custom-call | flops 8455716864 | bytes 7798784 | tf_op jit(solution)/shard_map/layer_inside/pallas_call | solution.py:487
  59.3 0.0 collective-permute-done.refs_1_
  59.4 0.0 collective-permute-done.1.refs_2_
  59.4 2.0 %layer_edges.1 = (bf16[8,2,64,256]{3,2,1,0:T(8,128)(2,1)S(1)}, f32[200,128]{1,0:T(8,128)S(1)}, f32[200,128]{1,0:T(8,128)S(1)}) custom-call(s32[1]{0:T(128)} %bitcast.side_ref.refs_0_, bf16[8,2,2,32,128]{4,3,2,1,0:T(8,128)(2,1)S(1)} %collective-permute-done.refs_1_, bf16[8,2,2,32,128]{4,3,2,1,0:T(8,128)(2,1)S(1)} %collective-permute-done.1.refs_2_, ...), custom_call_target="tpu_custom_call" | custom-call | flops 2818572288 | bytes 1458176 | tf_op jit(solution)/shard_map/layer_edges/pallas_call | solution.py:487
  61.4 4.8 %collective-permute-start.2 = (f32[200,128]{1,0:T(8,128)S(1)}, f32[200,128]{1,0:T(8,128)S(1)}, u32[]{:S(2)}, u32[]{:S(2)}) collective-permute-start(f32[200,128]{1,0:T(8,128)S(1)} %get-tuple-element.34), channel_id=1, source_target_pairs={{0,1},{1,0},{2,3},{3,2},{4,5},{5,4},{6,7},{7,6},{8,9},{9,8},{10,11... | collective-permute-start | bytes 307208 | tf_op jit(solution)/shard_map/ppermute | solution.py:500
  66.1 0.9 %collective-permute-done.2 = f32[200,128]{1,0:T(8,128)S(1)} collective-permute-done((f32[200,128]{1,0:T(8,128)S(1)}, f32[200,128]{1,0:T(8,128)S(1)}, u32[]{:S(2)}, u32[]{:S(2)}) %collective-permute-start.2) | collective-permute-done | bytes 102432 | tf_op jit(solution)/shard_map/ppermute | solution.py:500
  67.1 4.5 %collective-permute-start.3 = (f32[200,128]{1,0:T(8,128)S(1)}, f32[200,128]{1,0:T(8,128)S(1)}, u32[]{:S(2)}, u32[]{:S(2)}) collective-permute-start(f32[200,128]{1,0:T(8,128)S(1)} %add.12), channel_id=1, source_target_pairs={{0,2},{1,5},{2,0},{3,7},{4,6},{5,1},{6,4},{7,3},{8,10},{9,13},{10,... | collective-permute-start | bytes 307208 | tf_op jit(solution)/shard_map/ppermute | solution.py:507
  71.6 2.6 %collective-permute-done.3 = f32[200,128]{1,0:T(8,128)S(1)} collective-permute-done((f32[200,128]{1,0:T(8,128)S(1)}, f32[200,128]{1,0:T(8,128)S(1)}, u32[]{:S(2)}, u32[]{:S(2)}) %collective-permute-start.3) | collective-permute-done | bytes 102432 | tf_op jit(solution)/shard_map/ppermute | solution.py:507
  74.2 4.4 %collective-permute-start.4 = (f32[200,128]{1,0:T(8,128)S(1)}, f32[200,128]{1,0:T(8,128)S(1)}, u32[]{:S(2)}, u32[]{:S(2)}) collective-permute-start(f32[200,128]{1,0:T(8,128)S(1)} %add.13), channel_id=1, source_target_pairs={{0,4},{1,9},{2,6},{3,11},{4,0},{5,13},{6,2},{7,15},{8,12},{9,1},{1... | collective-permute-start | bytes 307208 | tf_op jit(solution)/shard_map/ppermute | solution.py:507
  78.6 1.7 %temporal_output.2.refs_3_ = bf16[8,2,64,1024]{3,2,1,0:T(8,128)(2,1)} custom-call(bf16[8,2,64,768]{3,2,1,0:T(8,128)(2,1)S(1)} %get-tuple-element.35.refs_0_, bf16[8,2,64,256]{3,2,1,0:T(8,128)(2,1)S(1)} %get-tuple-element.36.refs_1_, bf16[3,64,64]{2,1,0:T(8,128)(2,1)S(1)} %copy-done), custom_call_target="tpu_custom_call" | custom-call | flops 1207959552 | bytes 4194304 | tf_op jit(solution)/shard_map/temporal_output/pallas_call | solution.py:224
  80.3 1.5 %collective-permute-done.4 = f32[200,128]{1,0:T(8,128)S(1)} collective-permute-done((f32[200,128]{1,0:T(8,128)S(1)}, f32[200,128]{1,0:T(8,128)S(1)}, u32[]{:S(2)}, u32[]{:S(2)}) %collective-permute-start.4) | collective-permute-done | bytes 102432 | tf_op jit(solution)/shard_map/ppermute | solution.py:507
  81.8 3.1 %collective-permute-start.5 = (f32[200,128]{1,0:T(8,128)S(1)}, f32[200,128]{1,0:T(8,128)S(1)}, u32[]{:S(2)}, u32[]{:S(2)}) collective-permute-start(f32[200,128]{1,0:T(8,128)S(1)} %add.14), channel_id=1, source_target_pairs={{0,8},{1,3},{2,10},{3,1},{4,12},{5,7},{6,14},{7,5},{8,0},{9,11},{1... | collective-permute-start | bytes 307208 | tf_op jit(solution)/shard_map/ppermute | solution.py:507
  84.9 1.7 %temporal_output.3 = bf16[8,2,64,1024]{3,2,1,0:T(8,128)(2,1)} custom-call(bf16[8,2,64,768]{3,2,1,0:T(8,128)(2,1)S(1)} %get-tuple-element.35.refs_0_, bf16[8,2,64,256]{3,2,1,0:T(8,128)(2,1)S(1)} %get-tuple-element.36.refs_1_, bf16[3,64,64]{2,1,0:T(8,128)(2,1)S(1)} %copy-done, ...), custom_call_target="tpu_custom_call", output_to_operand_aliasing={{}: (3, {})} | custom-call | flops 1207959552 | bytes 4194304 | tf_op jit(solution)/shard_map/temporal_output/pallas_call | solution.py:224
  86.6 1.0 %collective-permute-done.5 = f32[200,128]{1,0:T(8,128)S(1)} collective-permute-done((f32[200,128]{1,0:T(8,128)S(1)}, f32[200,128]{1,0:T(8,128)S(1)}, u32[]{:S(2)}, u32[]{:S(2)}) %collective-permute-start.5) | collective-permute-done | bytes 102432 | tf_op jit(solution)/shard_map/ppermute | solution.py:507
  87.6 0.1 collective-permute-start.6
  87.6 1.3 %collective-permute-done.6.other_ref = f32[200,128]{1,0:T(8,128)S(1)} collective-permute-done((f32[200,128]{1,0:T(8,128)S(1)}, f32[200,128]{1,0:T(8,128)S(1)}, u32[]{:S(2)}, u32[]{:S(2)}) %collective-permute-start.6) | collective-permute-done | bytes 102432 | tf_op jit(solution)/shard_map/ppermute | solution.py:584
  88.9 0.9 unpack.1
  (5 shorter events, 0.1 us)
Async XLA Ops:
  3.2 7.6 %copy-start = (bf16[3,64,64]{2,1,0:T(8,128)(2,1)S(1)}, bf16[3,64,64]{2,1,0:T(8,128)(2,1)}, u32[]{:S(2)}) copy-start(bf16[3,64,64]{2,1,0:T(8,128)(2,1)} %refs_2_.3) | copy-start | bytes 73732
  3.2 7.6 %copy-start.1 = (bf16[9,64,64]{2,1,0:T(8,128)(2,1)S(1)}, bf16[9,64,64]{2,1,0:T(8,128)(2,1)}, u32[]{:S(2)}) copy-start(bf16[9,64,64]{2,1,0:T(8,128)(2,1)} %sw_ref.1) | copy-start | bytes 221188
  3.2 7.6 %copy-start.2 = (f32[64]{0:T(128)S(1)}, f32[64]{0:T(128)}, u32[]{:S(2)}) copy-start(f32[64]{0:T(128)} %param.7) | copy-start | bytes 772
  3.2 48.6 %all-to-all-start = ((bf16[16,2,8,32,128]{4,3,2,1,0:T(8,128)(2,1)}), bf16[16,2,8,32,128]{4,3,2,1,0:T(8,128)(2,1)S(1)}, u32[]{:S(2)}, u32[]{:S(2)}) async-start(bf16[16,2,8,32,128]{4,3,2,1,0:T(8,128)(2,1)} %pack.1), calls=%async_computation | async-start | bytes 4194304 | tf_op jit(solution)/shard_map/all_to_all | solution.py:554
  51.8 1.6 %copy-start.3 = (bf16[16,64,1024]{2,1,0:T(8,128)(2,1)S(1)}, bf16[16,64,1024]{2,1,0:T(8,128)(2,1)}, u32[]{:S(2)}) copy-start(bf16[16,64,1024]{2,1,0:T(8,128)(2,1)} %get-tuple-element.26) | copy-start | bytes 6291460
  51.9 7.5 %collective-permute-start = (bf16[8,2,2,32,128]{4,3,2,1,0:T(8,128)(2,1)S(1)}, bf16[8,2,2,32,128]{4,3,2,1,0:T(8,128)(2,1)S(1)}, u32[]{:S(2)}, u32[]{:S(2)}) collective-permute-start(bf16[8,2,2,32,128]{4,3,2,1,0:T(8,128)(2,1)S(1)} %get-tuple-element.24), channel_id=1, source_target_pairs={{0,1},{1,0},{2,3},{3,2},{4,5},{5,4},{6,7},{7,6},{8,9},{9,8},{10,11... | collective-permute-start | bytes 786440 | tf_op jit(solution)/shard_map/ppermute | solution.py:562
  52.7 6.6 %collective-permute-start.1 = (bf16[8,2,2,32,128]{4,3,2,1,0:T(8,128)(2,1)S(1)}, bf16[8,2,2,32,128]{4,3,2,1,0:T(8,128)(2,1)S(1)}, u32[]{:S(2)}, u32[]{:S(2)}) collective-permute-start(bf16[8,2,2,32,128]{4,3,2,1,0:T(8,128)(2,1)S(1)} %get-tuple-element.25), channel_id=1, source_target_pairs={{2,1},{4,3},{6,5},{8,7},{10,9},{12,11},{14,13},{1,2},{3,4},{5,6},{... | collective-permute-start | bytes 786440 | tf_op jit(solution)/shard_map/ppermute | solution.py:561
  61.4 5.7 %collective-permute-start.2 = (f32[200,128]{1,0:T(8,128)S(1)}, f32[200,128]{1,0:T(8,128)S(1)}, u32[]{:S(2)}, u32[]{:S(2)}) collective-permute-start(f32[200,128]{1,0:T(8,128)S(1)} %get-tuple-element.34), channel_id=1, source_target_pairs={{0,1},{1,0},{2,3},{3,2},{4,5},{5,4},{6,7},{7,6},{8,9},{9,8},{10,11... | collective-permute-start | bytes 307208 | tf_op jit(solution)/shard_map/ppermute | solution.py:500
  67.1 7.1 %collective-permute-start.3 = (f32[200,128]{1,0:T(8,128)S(1)}, f32[200,128]{1,0:T(8,128)S(1)}, u32[]{:S(2)}, u32[]{:S(2)}) collective-permute-start(f32[200,128]{1,0:T(8,128)S(1)} %add.12), channel_id=1, source_target_pairs={{0,2},{1,5},{2,0},{3,7},{4,6},{5,1},{6,4},{7,3},{8,10},{9,13},{10,... | collective-permute-start | bytes 307208 | tf_op jit(solution)/shard_map/ppermute | solution.py:507
  74.2 7.5 %collective-permute-start.4 = (f32[200,128]{1,0:T(8,128)S(1)}, f32[200,128]{1,0:T(8,128)S(1)}, u32[]{:S(2)}, u32[]{:S(2)}) collective-permute-start(f32[200,128]{1,0:T(8,128)S(1)} %add.13), channel_id=1, source_target_pairs={{0,4},{1,9},{2,6},{3,11},{4,0},{5,13},{6,2},{7,15},{8,12},{9,1},{1... | collective-permute-start | bytes 307208 | tf_op jit(solution)/shard_map/ppermute | solution.py:507
  81.8 5.8 %collective-permute-start.5 = (f32[200,128]{1,0:T(8,128)S(1)}, f32[200,128]{1,0:T(8,128)S(1)}, u32[]{:S(2)}, u32[]{:S(2)}) collective-permute-start(f32[200,128]{1,0:T(8,128)S(1)} %add.14), channel_id=1, source_target_pairs={{0,8},{1,3},{2,10},{3,1},{4,12},{5,7},{6,14},{7,5},{8,0},{9,11},{1... | collective-permute-start | bytes 307208 | tf_op jit(solution)/shard_map/ppermute | solution.py:507
  87.6 1.4 %collective-permute-start.6 = (f32[200,128]{1,0:T(8,128)S(1)}, f32[200,128]{1,0:T(8,128)S(1)}, u32[]{:S(2)}, u32[]{:S(2)}) collective-permute-start(f32[200,128]{1,0:T(8,128)S(1)} %add.15.mine_ref), channel_id=1, source_target_pairs={{0,1},{1,0},{2,3},{3,2},{4,5},{5,4},{6,7},{7,6},{8,9},{9,8},{10,11... | collective-permute-start | bytes 307208 | tf_op jit(solution)/shard_map/ppermute | solution.py:584
